TPU v7x, 32 devices: a whole 2x2x4 slice. The times are simulated.
32 devices in a mesh: pool: 4 (over y, core), expert: 8 (over z, x).
Axes of the slice: x: 2, y: 2, z: 4, core: 2. Of those that a mesh axis runs over, the one named last changes fastest.
Arguments:
- residual: bfloat16 [64, 2, 4096], P('expert'), may hold values from -6 to 6
- queries: bfloat16 [64, 2, 32, 128], P('expert', None, 'pool'), may hold values from -150 to 150
- kv_cache: bfloat16 [64, 512, 2, 2, 128], P('expert'), may hold values from -6 to 6
- kv_pages: bfloat16 [16, 8, 64, 2, 2, 128], P('pool', 'expert'), may hold values from -6 to 6
- cache_len: int32 [64], P('expert'), may hold values from 1 to 510, 16320 in all
- page_row: int32 [16, 8], P(None, 'expert'), may hold values from 0 to 7
- page_len: int32 [16, 8], P(None, 'expert'), may hold values from 1 to 64
- routes: int32 [64, 2, 8], P('expert'), may hold values from 0 to 15, all different within a row; in each aligned block of 16 rows (0 to 15, 16 to 31, ..., all dimensions but the last counted through in order) at most 12 rows name the same one
- route_weight: float32 [64, 2, 8], P('expert'), may hold values from 0.05 to 0.5
- out_weight: bfloat16 [4096, 4096], P('pool'), may hold values from -1.5 to 1.5
- gate_weight: bfloat16 [16, 4096, 1024], P('expert', None, 'pool'), may hold values from -0.09375 to 0.09375
- up_weight: bfloat16 [16, 4096, 1024], P('expert', None, 'pool'), may hold values from -0.09375 to 0.09375
- down_weight: bfloat16 [16, 1024, 4096], P('expert', 'pool'), may hold values from -0.375 to 0.375
Outputs:
- layer_out: bfloat16 [64, 2, 4096], P('expert')
Inputs may be any that keep to these rules, and one draw needn't show every extreme that they name: The row's two new tokens sit at positions cache_len and cache_len + 1 of its cache. The page belongs to row e * 8 + page_row of its group e. `routes`: a token names distinct experts; among the 16 new tokens of one device's rows no expert is named by more than 12 tokens.
All inputs are finite; a program needn't handle non-finite values. No bound on the sum of `cache_len` on one device may be relied on, other than what follows from the above.
Results may differ from a plain program's by a relative error of at most 0.028.
Values may be sent and summed in bfloat16 or wider, within the bound.
No kernel may reach another device: no remote copies, remote signals or barrier semaphores. Data moves between devices by JAX's collectives and lax.ppermute only.
A program may use at most 64 MiB of HBM per device.

v0:
```python
import functools
import math

import jax
import jax.numpy as jnp
from jax import lax
from jax.experimental import pallas as pl
from jax.experimental.pallas import tpu as pltpu
from jax.sharding import PartitionSpec as P


MIB = 1 << 20
LANES = 128
very_low = -1e30
cores = 2
near = 2
VMEM = pl.BlockSpec(memory_space=pltpu.VMEM)
HBM = pl.BlockSpec(memory_space=pltpu.HBM)
ANY = pl.BlockSpec(memory_space=pl.ANY)
float32 = jnp.float32
bfloat16 = jnp.bfloat16


def far_off(array):
    return pltpu.with_memory_space_constraint(array, pltpu.HBM)


def dot_t(a, b):
    return lax.dot_general(a, b, (((1,), (1,)), ((), ())), preferred_element_type=float32)


def dot(a, b):
    return jnp.dot(a, b, preferred_element_type=float32)


def slice_kernel(kv_heads, pages_hbm, own_ref, *rest):
    others, sem = rest[:-1], rest[-1]
    pool_size = lax.axis_size("pool")
    me = lax.axis_index("pool")
    copies = []
    for k, dest in enumerate((own_ref,) + others):
        head = (me ^ (k * cores)) * kv_heads // pool_size
        copies.append(pltpu.make_async_copy(pages_hbm.at[:, 0, :, head], dest, sem.at[k]))
    for copy in copies[::-1]:
        copy.start()
    for copy in copies:
        copy.wait()


def cache_kernel(
    scale, len_hbm, row_hbm, size_hbm, q_hbm, own_ref, kv_hbm, weight_hbm, residual_hbm,
    acc_ref, top_ref, total_ref, q_ref, owner_ref, send_ref, keep_ref, residual_ref,
    kv_ref, raw_ref, score_ref, low_ref, len_ref, row_ref, size_ref, small_sem, kv_sem, weight_sem,
):
    rows, length, kv_heads = kv_hbm.shape[:3]
    head_dim = kv_hbm.shape[4]
    pool_size = lax.axis_size("pool")
    me = lax.axis_index("pool")
    core = me % cores
    head = me * kv_heads // pool_size
    small = [
        pltpu.make_async_copy(len_hbm, len_ref, small_sem.at[0]),
        pltpu.make_async_copy(row_hbm, row_ref, small_sem.at[1]),
        pltpu.make_async_copy(size_hbm, size_ref, small_sem.at[2]),
        pltpu.make_async_copy(q_hbm, q_ref, small_sem.at[3]),
    ]
    for copy in small:
        copy.start()
    copies = [pltpu.make_async_copy(kv_hbm.at[r, :, head], kv_ref.at[r], kv_sem.at[r]) for r in range(rows)]
    for copy in copies:
        copy.start()
    chunks = weight_sem.shape[1]
    deep = weight_hbm.shape[0] // chunks
    half = send_ref.shape[1]
    mine = pl.ds(pl.multiple_of(core * half, half), half)
    theirs = pl.ds(pl.multiple_of((1 - core) * half, half), half)
    weights_in = [pltpu.make_async_copy(residual_hbm.at[:, :, mine], raw_ref, small_sem.at[4])]
    for side, (columns, target) in enumerate(((theirs, send_ref), (mine, keep_ref))):
        for n in range(chunks):
            part = pl.ds(n * deep, deep)
            weights_in.append(
                pltpu.make_async_copy(weight_hbm.at[part, columns], target.at[part], weight_sem.at[side, n])
            )
    for copy in weights_in:
        copy.start()
    for copy in small:
        copy.wait()
    everything = q_ref.shape[0]
    group = everything // rows
    steps = residual_hbm.shape[1]
    deep = 2 * length
    kv_rows = kv_ref.reshape(rows, deep, head_dim)
    page_rows = own_ref.shape[0]
    held = row_ref.shape[0] // pool_size
    span = page_rows // held
    page_lane = lax.broadcasted_iota(jnp.int32, (8, span), 1)
    page_key = jnp.where(page_lane % 2 == 0, page_lane // 2, span)
    owners = []
    for k in range(pool_size):
        source = me ^ (k * cores if k * cores < pool_size else (k * cores) % pool_size + 1)
        for i in range(held):
            page = source * held + i
            owners.append(jnp.where(page_key < size_ref[page], row_ref[page], -1))
    owner_ref[...] = jnp.concatenate(owners[held:], axis=1)
    own_owner = jnp.concatenate(owners[:held], axis=1)[:1]
    lane = lax.broadcasted_iota(jnp.int32, (1, deep), 1)
    key = jnp.where(lane % 2 == 0, lane // 2, 2 * length)
    step = lax.broadcasted_iota(jnp.int32, (group, 1), 0) // (group // steps)
    score_ref[:, deep:] = dot_t(q_ref[...], own_ref[...])
    here = [slice(r * group, (r + 1) * group) for r in range(rows)]
    for r in range(rows):
        copies[r].wait()
        score_ref[here[r], :deep] = dot_t(q_ref[here[r], :], kv_rows[r])
    for r in range(rows):
        scores = score_ref[here[r], :] * scale
        seen = jnp.concatenate(
            [key <= len_ref[r] + step, jnp.broadcast_to(own_owner == r, (group, page_rows))], axis=1
        )
        scores = jnp.where(seen, scores, very_low)
        top = jnp.max(scores, axis=1, keepdims=True)
        weights = jnp.where(seen, jnp.exp(scores - top), 0.0)
        total = jnp.sum(weights, axis=1, keepdims=True)
        low_ref[here[r], :] = pltpu.roll(weights, 1, 1).astype(bfloat16)
        top_ref[here[r], :] = jnp.broadcast_to(top, (group, top_ref.shape[1]))
        total_ref[here[r], :] = jnp.broadcast_to(total, (group, total_ref.shape[1]))
    acc_ref[...] = dot(low_ref[:, deep:], own_ref[...])
    for r in range(rows):
        acc_ref[here[r], :] += dot(low_ref[here[r], :deep], kv_rows[r])
    for copy in weights_in:
        copy.wait()
    first = jnp.where(me // cores == 0, 1.0, 0.0)
    residual_ref[...] = raw_ref.reshape(*residual_ref.shape)[...].astype(float32) * first


def page_kernel(heads, rows, scale, q_ref, acc_in, top_in, total_in, owner_ref, *rest):
    pages = rest[:-6]
    weight_ref, low_ref, send_ref, score_ref, chance_ref, flat_ref = rest[-6:]
    everything, _ = q_ref.shape
    group = everything // rows
    size = pages[0].shape[0]
    for n, page in enumerate(pages):
        score_ref[:, n * size : (n + 1) * size] = dot_t(q_ref[...], page[...])
    owner = owner_ref[:1, :]
    for r in range(rows):
        here = slice(r * group, (r + 1) * group)
        seen = jnp.broadcast_to(owner == r, (group, owner.shape[1]))
        scores = jnp.where(seen, score_ref[here, :] * scale, very_low)
        top = jnp.maximum(top_in[here, :], jnp.max(scores, axis=1, keepdims=True))
        weights = jnp.where(seen, jnp.exp(scores - top[:, :1]), 0.0)
        shrink = jnp.exp(top_in[here, :] - top)
        total = total_in[here, :] * shrink + jnp.sum(weights, axis=1, keepdims=True)
        chance_ref[here, :] = pltpu.roll(weights, 1, 1).astype(bfloat16)
        inverse = 1.0 / total
        flat_ref[0, here, :] = inverse
        flat_ref[1, here, :] = acc_in[here, :] * shrink * inverse
    mixed = dot(chance_ref[:, :size], pages[0][...])
    for n in range(1, len(pages)):
        mixed = mixed + dot(chance_ref[:, n * size : (n + 1) * size], pages[n][...])
    flat_ref[1] = flat_ref[1] + mixed * flat_ref[0]
    tokens = everything // heads
    low = jnp.concatenate(
        [flat_ref[1, pl.ds(h, tokens, stride=heads), :].astype(bfloat16) for h in range(heads)], axis=1
    )
    low_ref[...] = low
    send_ref[...] = dot(low, weight_ref[...]).astype(bfloat16)


def project_kernel(low_ref, weight_ref, residual_ref, keep_ref):
    keep_ref[...] = dot(low_ref[...], weight_ref[...]) + residual_ref[...]


def expert_kernel(own_ref, other_ref, gate_ref, up_ref, down_ref, act_ref, send_ref):
    half = send_ref.shape[1]
    own = own_ref[:, :half]
    other = other_ref[:, :half]
    table = own_ref[:, half:].astype(float32)
    lane = lax.broadcasted_iota(jnp.int32, table.shape, 1)
    core = lax.axis_index("pool") % cores
    first = pl.ds(pl.multiple_of(core * half, half), half)
    second = pl.ds(pl.multiple_of((1 - core) * half, half), half)
    experts, _, units = gate_ref.shape
    everyone = experts * lax.axis_size("expert")
    for j in range(experts):
        mine = lax.axis_index("expert") * experts + j
        weight = jnp.sum(
            jnp.where((lane == mine) | (lane == mine + everyone), table, 0.0), axis=1, keepdims=True
        )
        gate = dot(own, gate_ref[j, first, :]) + dot(other, gate_ref[j, second, :])
        up = dot(own, up_ref[j, first, :]) + dot(other, up_ref[j, second, :])
        active = gate / (1.0 + jnp.exp(-gate)) * up
        act_ref[:, j * units : (j + 1) * units] = (active * weight).astype(bfloat16)
    total = 0.0
    for j in range(experts):
        total = total + dot(act_ref[:, j * units : (j + 1) * units], down_ref[j, :, second])
    send_ref[...] = total.astype(bfloat16)


def down_kernel(act_ref, down_ref, keep_ref):
    half = keep_ref.shape[1]
    experts, units, _ = down_ref.shape
    core = lax.axis_index("pool") % cores
    first = pl.ds(pl.multiple_of(core * half, half), half)
    total = 0.0
    for j in range(experts):
        total = total + dot(act_ref[:, j * units : (j + 1) * units], down_ref[j, :, first])
    keep_ref[...] = total


def finish_kernel(mine_ref, theirs_ref, out_ref):
    tokens, half = mine_ref.shape
    core = lax.axis_index("pool") % cores
    flat = out_ref.reshape(tokens, out_ref.shape[2])
    flat[:, pl.ds(pl.multiple_of(core * half, half), half)] = mine_ref[...]
    flat[:, pl.ds(pl.multiple_of((1 - core) * half, half), half)] = theirs_ref[...]


def call(kernel, outs, specs, scratch=(), vmem=16, flops=0, bytes_accessed=0, **kw):
    return pl.pallas_call(
        kernel,
        out_shape=outs,
        in_specs=specs,
        out_specs=jax.tree.map(lambda _: VMEM, outs),
        scratch_shapes=scratch,
        compiler_params=pltpu.CompilerParams(vmem_limit_bytes=vmem * MIB),
        cost_estimate=pl.CostEstimate(flops=flops, bytes_accessed=bytes_accessed, transcendentals=0),
        **kw,
    )


def per_device(
    residual,
    queries,
    kv_cache,
    kv_pages,
    cache_len,
    page_row,
    page_len,
    routes,
    route_weight,
    out_weight,
    gate_weight,
    up_weight,
    down_weight,
):
    pool_size = lax.axis_size("pool")
    expert_size = lax.axis_size("expert")
    outer, far = pool_size // cores, expert_size // near

    def swap(value, pool_flip=0, expert_flip=0):
        pairs = []
        for p in range(pool_size):
            for e in range(expert_size):
                pairs.append((p * expert_size + e, (p ^ pool_flip) * expert_size + (e ^ expert_flip)))
        return lax.ppermute(value, ("pool", "expert"), pairs)

    rows, steps, heads, head_dim = queries.shape
    length, kv_heads = kv_cache.shape[1:3]
    held, _, page_size = kv_pages.shape[:3]
    width = residual.shape[2]
    half = width // cores
    tokens = rows * steps
    scale = 1.0 / math.sqrt(head_dim)

    page_rows = held * page_size * 2
    piece = jax.ShapeDtypeStruct((held, page_size, 2, head_dim), bfloat16)
    sliced = call(
        functools.partial(slice_kernel, kv_heads),
        (piece,) * outer,
        [HBM],
        scratch=[pltpu.SemaphoreType.DMA((outer,))],
        vmem=4,
        bytes_accessed=2 * kv_pages.size,
    )(far_off(kv_pages))
    sliced = [p.reshape(page_rows, head_dim) for p in sliced]
    sets = [sliced[0]]
    for k in range(1, outer):
        sets.append(swap(sliced[k], k * cores))
    for k in range(outer):
        sets.append(swap(sliced[k], k * cores + 1))

    group = steps * heads
    everything = rows * group
    stat = jax.ShapeDtypeStruct((everything, head_dim), float32)
    weight_half = jax.ShapeDtypeStruct((out_weight.shape[0], half), bfloat16)
    q_shape = jax.ShapeDtypeStruct((everything, head_dim), bfloat16)
    other_lanes = (pool_size - 1) * page_rows
    lanes = 2 * length + page_rows
    acc, top, total, q, owner, weight_send, weight_keep, own_residual = call(
        functools.partial(cache_kernel, scale),
        (
            stat, stat, stat, q_shape, jax.ShapeDtypeStruct((8, other_lanes), jnp.int32), weight_half, weight_half,
            jax.ShapeDtypeStruct((tokens, half), float32),
        ),
        [HBM] * 4 + [VMEM] + [HBM] * 3,
        scratch=[
            pltpu.VMEM((rows, length, 2, head_dim), bfloat16),
            pltpu.VMEM((rows, steps, half), bfloat16),
            pltpu.VMEM((everything, lanes), float32),
            pltpu.VMEM((everything, lanes), bfloat16),
            pltpu.SMEM((rows,), jnp.int32),
            pltpu.SMEM(page_row[:, 0].shape, jnp.int32),
            pltpu.SMEM(page_len[:, 0].shape, jnp.int32),
            pltpu.SemaphoreType.DMA((5,)),
            pltpu.SemaphoreType.DMA((rows,)),
            pltpu.SemaphoreType.DMA((2, 4)),
        ],
        vmem=24,
        flops=4 * everything * lanes * head_dim,
        bytes_accessed=kv_cache.size + out_weight.size * 2,
    )(
        far_off(cache_len), far_off(page_row[:, 0]), far_off(page_len[:, 0]),
        far_off(queries.reshape(everything, head_dim)), sets[0], far_off(kv_cache), far_off(out_weight),
        far_off(residual),
    )
    low, send = call(
        functools.partial(page_kernel, heads, rows, scale),
        (
            jax.ShapeDtypeStruct((tokens, heads * head_dim), bfloat16),
            jax.ShapeDtypeStruct((tokens, half), bfloat16),
        ),
        [VMEM] * (5 + pool_size),
        scratch=[
            pltpu.VMEM((everything, other_lanes), float32),
            pltpu.VMEM((everything, other_lanes), bfloat16),
            pltpu.VMEM((2, everything, head_dim), float32),
        ],
        flops=2 * tokens * heads * head_dim * half,
    )(q, acc, top, total, owner, *sets[1:], weight_send)
    arrived = swap(send, 1)
    keep = call(
        project_kernel, jax.ShapeDtypeStruct((tokens, half), float32), [VMEM] * 3,
        flops=2 * tokens * heads * head_dim * half,
    )(low, weight_keep, own_residual)

    experts = gate_weight.shape[0] * expert_size
    wide = -(-2 * experts // LANES) * LANES
    routes = routes.reshape(tokens, -1)
    named = routes[:, :, None] == jnp.arange(wide, dtype=jnp.int32) % experts
    table = jnp.sum(jnp.where(named, route_weight.reshape(tokens, -1, 1), 0.0), axis=1)
    coarse = lax.reduce_precision(table, 8, 7)
    table = jnp.where(jnp.arange(wide) < experts, coarse, jnp.where(jnp.arange(wide) < 2 * experts, table - coarse, 0.0))

    partial = keep + arrived.astype(float32)
    summed = partial.astype(bfloat16)
    hidden = summed.astype(float32)
    for k in range(1, outer):
        hidden = hidden + swap(summed, k * cores).astype(float32)
    message = jnp.concatenate([hidden, table], axis=1).astype(bfloat16)
    gate_near, up_near, down_near = gate_weight, up_weight, down_weight
    units = gate_weight.shape[0] * gate_weight.shape[2]
    result = 0.0
    flips = list(range(far - 1, 0, -1))
    same = [message]
    for k in flips:
        same.append(swap(message, 0, k * near))
    beside = swap(message, 0, 1)
    same = jnp.concatenate(same, axis=0)
    rest = swap(same[tokens:], 0, 1)
    gathered = (same, jnp.concatenate([beside, rest], axis=0))
    for index, own in enumerate(gathered):
        other = swap(own, 1)
        batch = [k * near + index for k in [0] + flips]
        here = len(batch) * tokens
        act, outgoing = call(
            expert_kernel,
            (jax.ShapeDtypeStruct((here, units), bfloat16), jax.ShapeDtypeStruct((here, half), bfloat16)),
            [VMEM] * 5,
            flops=5 * here * width * units,
        )(own, other, gate_near, up_near, down_near)
        incoming = swap(outgoing, 1)
        kept = call(
            down_kernel, jax.ShapeDtypeStruct((here, half), float32), [VMEM] * 2, flops=2 * here * half * units
        )(act, down_near)
        total = kept + incoming.astype(float32)
        for n, k in enumerate(batch):
            part = total[n * tokens : (n + 1) * tokens]
            if k:
                part = swap(part.astype(bfloat16), 0, k).astype(float32)
            result = result + part
    outcome = result.astype(bfloat16)
    result = hidden + result
    for k in range(1, outer):
        result = result + swap(outcome, k * cores).astype(float32)
    mine = result.astype(bfloat16)
    theirs = swap(mine, 1)
    return call(
        finish_kernel, jax.ShapeDtypeStruct(residual.shape, bfloat16), [VMEM] * 2, vmem=4, bytes_accessed=4 * residual.size
    )(mine, theirs)


def solution(mesh):
    return jax.shard_map(
        per_device,
        mesh=mesh,
        in_specs=(
            P("expert", None, None),
            P("expert", None, "pool", None),
            P("expert", None, None, None, None),
            P("pool", "expert", None, None, None, None),
            P("expert"),
            P(None, "expert"),
            P(None, "expert"),
            P("expert", None, None),
            P("expert", None, None),
            P("pool", None),
            P("expert", None, "pool"),
            P("expert", None, "pool"),
            P("expert", "pool", None),
        ),
        out_specs=P("expert", None, None),
        check_vma=False,
    )
```

profile of v0, /device:TPU:0, one launch (start us, length us, event | category | flops | bytes accessed | tf_op | source)
XLA Modules:
  0.0 63.4 jit_solution(3821178167736491699)
XLA Ops:
  0.0 1.0 %shard_map.127 = (bf16[4,64,2,128]{3,2,1,0:T(2,128)(2,1)S(1)}, bf16[4,64,2,128]{3,2,1,0:T(2,128)(2,1)S(1)}) custom-call(bf16[4,1,64,2,2,128]{5,4,3,2,1,0:T(2,128)(2,1)} %pages_hbm.1), custom_call_target="tpu_custom_call" | custom-call | bytes 262144 | tf_op jit(solution)/shard_map/pallas_call | solution.py:266
  1.0 2.5 %collective-permute-start.2 = (bf16[512,128]{1,0:T(8,128)(2,1)S(1)}, bf16[512,128]{1,0:T(8,128)(2,1)S(1)}, u32[]{:S(2)}, u32[]{:S(2)}) collective-permute-start(bf16[512,128]{1,0:T(8,128)(2,1)S(1)} %bitcast.9), channel_id=1, source_target_pairs={{0,24},{1,25},{2,26},{3,27},{4,28},{5,29},{6,30},{7,31},{8,16},{9,... | collective-permute-start | bytes 393224 | tf_op jit(solution)/shard_map/ppermute | solution.py:254
  3.5 0.6 %collective-permute-start = (bf16[512,128]{1,0:T(8,128)(2,1)S(1)}, bf16[512,128]{1,0:T(8,128)(2,1)S(1)}, u32[]{:S(2)}, u32[]{:S(2)}) collective-permute-start(bf16[512,128]{1,0:T(8,128)(2,1)S(1)} %bitcast.10), channel_id=1, source_target_pairs={{0,16},{1,17},{2,18},{3,19},{4,20},{5,21},{6,22},{7,23},{8,24},{9,... | collective-permute-start | bytes 393224 | tf_op jit(solution)/shard_map/ppermute | solution.py:254
  4.1 0.0 collective-permute-start.1
  4.2 7.2 %shard_map.128 = (f32[128,128]{1,0:T(8,128)S(1)}, f32[128,128]{1,0:T(8,128)S(1)}, f32[128,128]{1,0:T(8,128)S(1)}, bf16[128,128]{1,0:T(8,128)(2,1)S(1)}, s32[8,15...) custom-call(s32[8]{0:T(128)} %len_hbm.1, ...), custom_call_target="tpu_custom_call" | custom-call | flops 100663296 | bytes 10485760 | tf_op jit(solution)/shard_map/pallas_call | solution.py:288
  11.4 0.0 copy-done.3
  11.4 0.0 copy-done.4
  11.4 0.1 select_reduce_fusion
  11.5 0.0 collective-permute-done.2.rest_2_
  11.5 0.0 collective-permute-done.rest_0_
  11.6 0.0 collective-permute-done.1.rest_1_
  11.6 0.0 copy-start.1
  11.6 1.4 %shard_map.129 = (bf16[16,1024]{1,0:T(8,128)(2,1)S(1)}, bf16[16,2048]{1,0:T(8,128)(2,1)S(1)}) custom-call(bf16[128,128]{1,0:T(8,128)(2,1)S(1)} %get-tuple-element.22.q_ref, f32[128,128]{1,0:T(8,128)S(1)} %get-tuple-element.23.acc_in, f32[128,128]{1,0:T(8,128)S(1)} %get-tuple-element.24.top_in, f32[128,128]{1,0:T(8,128)S(1)} %get-tuple-element.25.total_in, ...), custom_call_target="tpu_custom_call" | custom-call | flops 67108864 | tf_op jit(solution)/shard_map/pallas_call | solution.py:315
  13.0 0.5 collective-permute-start.3
  13.5 0.6 %shard_map.130 = f32[16,2048]{1,0:T(8,128)S(1)} custom-call(bf16[16,1024]{1,0:T(8,128)(2,1)S(1)} %get-tuple-element.29.low_ref, bf16[1024,2048]{1,0:T(8,128)(2,1)S(1)} %get-tuple-element.30.weight_ref, f32[16,2048]{1,0:T(8,128)S(1)} %get-tuple-element.31.residual_ref), custom_call_target="tpu_custom_call" | custom-call | flops 67108864 | tf_op jit(solution)/shard_map/pallas_call | solution.py:330
  14.1 0.2 collective-permute-done.3
  14.4 1.7 %collective-permute-start.4 = (bf16[16,2048]{1,0:T(8,128)(2,1)S(1)}, bf16[16,2048]{1,0:T(8,128)(2,1)S(1)}, u32[]{:S(2)}, u32[]{:S(2)}) collective-permute-start(bf16[16,2048]{1,0:T(8,128)(2,1)S(1)} %add_convert_fusion.2), channel_id=1, source_target_pairs={{0,16},{1,17},{2,18},{3,19},{4,20},{5,21},{6,22},{7,23},{8,24},{9,... | collective-permute-start | bytes 196616 | tf_op jit(solution)/shard_map/ppermute | solution.py:254
  16.1 2.7 %collective-permute-done.4 = bf16[16,2048]{1,0:T(8,128)(2,1)S(1)} collective-permute-done((bf16[16,2048]{1,0:T(8,128)(2,1)S(1)}, bf16[16,2048]{1,0:T(8,128)(2,1)S(1)}, u32[]{:S(2)}, u32[]{:S(2)}) %collective-permute-start.4) | collective-permute-done | bytes 65568 | tf_op jit(solution)/shard_map/ppermute | solution.py:254
  18.8 1.7 %collective-permute-start.7 = (bf16[16,2176]{1,0:T(8,128)(2,1)S(1)}, bf16[16,2176]{1,0:T(8,128)(2,1)S(1)}, u32[]{:S(2)}, u32[]{:S(2)}) collective-permute-start(bf16[16,2176]{1,0:T(8,128)(2,1)S(1)} %pad_maximum_fusion.2), channel_id=1, source_target_pairs={{0,2},{1,3},{2,0},{3,1},{4,6},{5,7},{6,4},{7,5},{8,10},{9,11},{10,... | collective-permute-start | bytes 208904 | tf_op jit(solution)/shard_map/ppermute | solution.py:254
  20.5 2.6 %collective-permute-start.6 = (bf16[16,2176]{1,0:T(8,128)(2,1)S(1)}, bf16[16,2176]{1,0:T(8,128)(2,1)S(1)}, u32[]{:S(2)}, u32[]{:S(2)}) collective-permute-start(bf16[16,2176]{1,0:T(8,128)(2,1)S(1)} %pad_maximum_fusion.2), channel_id=1, source_target_pairs={{0,4},{1,5},{2,6},{3,7},{4,0},{5,1},{6,2},{7,3},{8,12},{9,13},{10,... | collective-permute-start | bytes 208904 | tf_op jit(solution)/shard_map/ppermute | solution.py:254
  23.1 0.2 collective-permute-start.5
  23.3 1.5 %collective-permute-start.13 = (bf16[16,2176]{1,0:T(8,128)(2,1)S(1)}, bf16[16,2176]{1,0:T(8,128)(2,1)S(1)}, u32[]{:S(2)}, u32[]{:S(2)}) collective-permute-start(bf16[16,2176]{1,0:T(8,128)(2,1)S(1)} %pad_maximum_fusion.2), channel_id=1, source_target_pairs={{0,1},{1,0},{2,3},{3,2},{4,5},{5,4},{6,7},{7,6},{8,9},{9,8},{10,11... | collective-permute-start | bytes 208904 | tf_op jit(solution)/shard_map/ppermute | solution.py:254
  24.8 0.0 collective-permute-done.7
  24.8 2.5 %collective-permute-done.6 = bf16[16,2176]{1,0:T(8,128)(2,1)S(1)} collective-permute-done((bf16[16,2176]{1,0:T(8,128)(2,1)S(1)}, bf16[16,2176]{1,0:T(8,128)(2,1)S(1)}, u32[]{:S(2)}, u32[]{:S(2)}) %collective-permute-start.6) | collective-permute-done | bytes 69664 | tf_op jit(solution)/shard_map/ppermute | solution.py:254
  27.3 1.9 %collective-permute-done.5 = bf16[16,2176]{1,0:T(8,128)(2,1)S(1)} collective-permute-done((bf16[16,2176]{1,0:T(8,128)(2,1)S(1)}, bf16[16,2176]{1,0:T(8,128)(2,1)S(1)}, u32[]{:S(2)}, u32[]{:S(2)}) %collective-permute-start.5) | collective-permute-done | bytes 69664 | tf_op jit(solution)/shard_map/ppermute | solution.py:254
  29.2 1.6 %collective-permute-start.14 = (bf16[48,2176]{1,0:T(8,128)(2,1)S(1)}, bf16[48,2176]{1,0:T(8,128)(2,1)S(1)}, u32[]{:S(2)}, u32[]{:S(2)}) collective-permute-start(bf16[48,2176]{1,0:T(8,128)(2,1)S(1)} %pad_maximum_fusion.1), channel_id=1, source_target_pairs={{0,1},{1,0},{2,3},{3,2},{4,5},{5,4},{6,7},{7,6},{8,9},{9,8},{10,11... | collective-permute-start | bytes 626696 | tf_op jit(solution)/shard_map/ppermute | solution.py:254
  30.8 0.1 collective-permute-start.8
  30.9 0.0 collective-permute-done.13
  30.9 4.2 %collective-permute-done.14 = bf16[48,2176]{1,0:T(8,128)(2,1)S(1)} collective-permute-done((bf16[48,2176]{1,0:T(8,128)(2,1)S(1)}, bf16[48,2176]{1,0:T(8,128)(2,1)S(1)}, u32[]{:S(2)}, u32[]{:S(2)}) %collective-permute-start.14) | collective-permute-done | bytes 208928 | tf_op jit(solution)/shard_map/ppermute | solution.py:254
  35.1 0.1 collective-permute-start.15
  35.2 0.0 collective-permute-done.8.other_ref
  35.2 0.0 copy-done.2
  35.2 0.0 copy-done.1
  35.2 0.0 copy-done
  35.2 2.0 %shard_map.131 = (bf16[64,512]{1,0:T(8,128)(2,1)S(1)}, bf16[64,2048]{1,0:T(8,128)(2,1)S(1)}) custom-call(bf16[64,2176]{1,0:T(8,128)(2,1)S(1)} %pad_maximum_fusion.own_ref, bf16[64,2176]{1,0:T(8,128)(2,1)S(1)} %collective-permute-done.8.other_ref, bf16[2,4096,256]{2,1,0:T(8,128)(2,1)S(1)} %copy-done.1, bf16[2,4096,256]{2,1,0:T(8,128)(2,1)S(1)} %copy-done.2, ...), custom_call_target="tpu_custom_call" | custom-call | flops 671088640 | tf_op jit(solution)/shard_map/pallas_call | solution.py:364
  37.3 0.5 collective-permute-start.9
  37.8 0.5 shard_map.132
  38.3 0.0 collective-permute-done.15.other_ref
  38.3 2.0 %shard_map.133 = (bf16[64,512]{1,0:T(8,128)(2,1)S(1)}, bf16[64,2048]{1,0:T(8,128)(2,1)S(1)}) custom-call(bf16[64,2176]{1,0:T(8,128)(2,1)S(1)} %constant_dynamic-update-slice_fusion.own_ref, bf16[64,2176]{1,0:T(8,128)(2,1)S(1)} %collective-permute-done.15.other_ref, bf16[2,4096,256]{2,1,0:T(8,128)(2,1)S(1)} %copy-done.1, bf16[2,4096,256]{2,1,0:T(8,128)(2,1)S(1)} %copy-done.2, ...), custom_call_target="tpu_custom_call" | custom-call | flops 671088640 | tf_op jit(solution)/shard_map/pallas_call | solution.py:364
  40.3 0.1 collective-permute-start.16
  40.4 0.5 shard_map.134
  40.9 0.0 collective-permute-done.9
  40.9 0.1 fusion.11
  41.0 1.4 %collective-permute-start.10 = (bf16[16,2048]{1,0:T(8,128)(2,1)S(1)}, bf16[16,2048]{1,0:T(8,128)(2,1)S(1)}, u32[]{:S(2)}, u32[]{:S(2)}) collective-permute-start(bf16[16,2048]{1,0:T(8,128)(2,1)S(1)} %get-tuple-element.41), channel_id=1, source_target_pairs={{0,6},{1,7},{2,4},{3,5},{4,2},{5,3},{6,0},{7,1},{8,14},{9,15},{10,... | collective-permute-start | bytes 196616 | tf_op jit(solution)/shard_map/ppermute | solution.py:254
  42.4 0.4 collective-permute-start.12
  42.8 2.7 %collective-permute-start.11 = (bf16[16,2048]{1,0:T(8,128)(2,1)S(1)}, bf16[16,2048]{1,0:T(8,128)(2,1)S(1)}, u32[]{:S(2)}, u32[]{:S(2)}) collective-permute-start(bf16[16,2048]{1,0:T(8,128)(2,1)S(1)} %get-tuple-element.43), channel_id=1, source_target_pairs={{0,4},{1,5},{2,6},{3,7},{4,0},{5,1},{6,2},{7,3},{8,12},{9,13},{10,... | collective-permute-start | bytes 196616 | tf_op jit(solution)/shard_map/ppermute | solution.py:254
  45.5 0.0 collective-permute-done.16
  45.5 1.6 %collective-permute-start.17 = (bf16[16,2048]{1,0:T(8,128)(2,1)S(1)}, bf16[16,2048]{1,0:T(8,128)(2,1)S(1)}, u32[]{:S(2)}, u32[]{:S(2)}) collective-permute-start(bf16[16,2048]{1,0:T(8,128)(2,1)S(1)} %get-tuple-element.44), channel_id=1, source_target_pairs={{0,1},{1,0},{2,3},{3,2},{4,5},{5,4},{6,7},{7,6},{8,9},{9,8},{10,11... | collective-permute-start | bytes 196616 | tf_op jit(solution)/shard_map/ppermute | solution.py:254
  47.1 0.0 collective-permute-start.20
  47.1 0.8 %collective-permute-done.10 = bf16[16,2048]{1,0:T(8,128)(2,1)S(1)} collective-permute-done((bf16[16,2048]{1,0:T(8,128)(2,1)S(1)}, bf16[16,2048]{1,0:T(8,128)(2,1)S(1)}, u32[]{:S(2)}, u32[]{:S(2)}) %collective-permute-start.10) | collective-permute-done | bytes 65568 | tf_op jit(solution)/shard_map/ppermute | solution.py:254
  47.9 2.0 %collective-permute-start.19 = (bf16[16,2048]{1,0:T(8,128)(2,1)S(1)}, bf16[16,2048]{1,0:T(8,128)(2,1)S(1)}, u32[]{:S(2)}, u32[]{:S(2)}) collective-permute-start(bf16[16,2048]{1,0:T(8,128)(2,1)S(1)} %get-tuple-element.46), channel_id=1, source_target_pairs={{0,5},{1,4},{2,7},{3,6},{4,1},{5,0},{6,3},{7,2},{8,13},{9,12},{10,... | collective-permute-start | bytes 196616 | tf_op jit(solution)/shard_map/ppermute | solution.py:254
  49.9 0.0 collective-permute-done.12
  49.9 2.6 %collective-permute-start.18 = (bf16[16,2048]{1,0:T(8,128)(2,1)S(1)}, bf16[16,2048]{1,0:T(8,128)(2,1)S(1)}, u32[]{:S(2)}, u32[]{:S(2)}) collective-permute-start(bf16[16,2048]{1,0:T(8,128)(2,1)S(1)} %get-tuple-element.47), channel_id=1, source_target_pairs={{0,7},{1,6},{2,5},{3,4},{4,3},{5,2},{6,1},{7,0},{8,15},{9,14},{10,... | collective-permute-start | bytes 196616 | tf_op jit(solution)/shard_map/ppermute | solution.py:254
  52.5 0.0 collective-permute-done.11
  52.5 0.0 collective-permute-done.17
  52.5 0.3 collective-permute-done.20
  52.9 2.9 %collective-permute-done.19 = bf16[16,2048]{1,0:T(8,128)(2,1)S(1)} collective-permute-done((bf16[16,2048]{1,0:T(8,128)(2,1)S(1)}, bf16[16,2048]{1,0:T(8,128)(2,1)S(1)}, u32[]{:S(2)}, u32[]{:S(2)}) %collective-permute-start.19) | collective-permute-done | bytes 65568 | tf_op jit(solution)/shard_map/ppermute | solution.py:254
  55.7 1.2 %collective-permute-done.18 = bf16[16,2048]{1,0:T(8,128)(2,1)S(1)} collective-permute-done((bf16[16,2048]{1,0:T(8,128)(2,1)S(1)}, bf16[16,2048]{1,0:T(8,128)(2,1)S(1)}, u32[]{:S(2)}, u32[]{:S(2)}) %collective-permute-start.18) | collective-permute-done | bytes 65568 | tf_op jit(solution)/shard_map/ppermute | solution.py:254
  56.9 0.1 fusion.9
  57.0 1.5 %collective-permute-start.21 = (bf16[16,2048]{1,0:T(8,128)(2,1)S(1)}, bf16[16,2048]{1,0:T(8,128)(2,1)S(1)}, u32[]{:S(2)}, u32[]{:S(2)}) collective-permute-start(bf16[16,2048]{1,0:T(8,128)(2,1)S(1)} %get-tuple-element.37), channel_id=1, source_target_pairs={{0,16},{1,17},{2,18},{3,19},{4,20},{5,21},{6,22},{7,23},{8,24},{9,... | collective-permute-start | bytes 196616 | tf_op jit(solution)/shard_map/ppermute | solution.py:254
  58.5 2.8 %collective-permute-done.21 = bf16[16,2048]{1,0:T(8,128)(2,1)S(1)} collective-permute-done((bf16[16,2048]{1,0:T(8,128)(2,1)S(1)}, bf16[16,2048]{1,0:T(8,128)(2,1)S(1)}, u32[]{:S(2)}, u32[]{:S(2)}) %collective-permute-start.21) | collective-permute-done | bytes 65568 | tf_op jit(solution)/shard_map/ppermute | solution.py:254
  61.4 0.1 collective-permute-start.22
  61.5 1.2 %collective-permute-done.22.theirs_ref = bf16[16,2048]{1,0:T(8,128)(2,1)S(1)} collective-permute-done((bf16[16,2048]{1,0:T(8,128)(2,1)S(1)}, bf16[16,2048]{1,0:T(8,128)(2,1)S(1)}, u32[]{:S(2)}, u32[]{:S(2)}) %collective-permute-start.22) | collective-permute-done | bytes 65568 | tf_op jit(solution)/shard_map/ppermute | solution.py:254
  62.7 0.7 %shard_map.135 = bf16[8,2,4096]{2,1,0:T(2,128)(2,1)} custom-call(bf16[16,2048]{1,0:T(8,128)(2,1)S(1)} %add_convert_fusion.1.mine_ref, bf16[16,2048]{1,0:T(8,128)(2,1)S(1)} %collective-permute-done.22.theirs_ref), custom_call_target="tpu_custom_call" | custom-call | bytes 262144 | tf_op jit(solution)/shard_map/pallas_call | solution.py:386
  (18 shorter events, 0.2 us)
Async XLA Ops:
  1.0 10.5 %collective-permute-start.2 = (bf16[512,128]{1,0:T(8,128)(2,1)S(1)}, bf16[512,128]{1,0:T(8,128)(2,1)S(1)}, u32[]{:S(2)}, u32[]{:S(2)}) collective-permute-start(bf16[512,128]{1,0:T(8,128)(2,1)S(1)} %bitcast.9), channel_id=1, source_target_pairs={{0,24},{1,25},{2,26},{3,27},{4,28},{5,29},{6,30},{7,31},{8,16},{9,... | collective-permute-start | bytes 393224 | tf_op jit(solution)/shard_map/ppermute | solution.py:254
  3.5 8.1 %collective-permute-start = (bf16[512,128]{1,0:T(8,128)(2,1)S(1)}, bf16[512,128]{1,0:T(8,128)(2,1)S(1)}, u32[]{:S(2)}, u32[]{:S(2)}) collective-permute-start(bf16[512,128]{1,0:T(8,128)(2,1)S(1)} %bitcast.10), channel_id=1, source_target_pairs={{0,16},{1,17},{2,18},{3,19},{4,20},{5,21},{6,22},{7,23},{8,24},{9,... | collective-permute-start | bytes 393224 | tf_op jit(solution)/shard_map/ppermute | solution.py:254
  4.1 7.4 %collective-permute-start.1 = (bf16[512,128]{1,0:T(8,128)(2,1)S(1)}, bf16[512,128]{1,0:T(8,128)(2,1)S(1)}, u32[]{:S(2)}, u32[]{:S(2)}) collective-permute-start(bf16[512,128]{1,0:T(8,128)(2,1)S(1)} %bitcast.7), channel_id=1, source_target_pairs={{0,8},{1,9},{2,10},{3,11},{4,12},{5,13},{6,14},{7,15},{8,0},{9,1},... | collective-permute-start | bytes 393224 | tf_op jit(solution)/shard_map/ppermute | solution.py:254
  4.2 7.2 %copy-start.3 = (f32[8,2,8]{2,1,0:T(2,128)S(1)}, f32[8,2,8]{2,1,0:T(2,128)}, u32[]{:S(2)}) copy-start(f32[8,2,8]{2,1,0:T(2,128)} %param.21) | copy-start | bytes 1540
  4.2 7.2 %copy-start.4 = (s32[8,2,8]{2,1,0:T(2,128)S(1)}, s32[8,2,8]{2,1,0:T(2,128)}, u32[]{:S(2)}) copy-start(s32[8,2,8]{2,1,0:T(2,128)} %param.20) | copy-start | bytes 1540
  4.2 31.0 %copy-start.2 = (bf16[2,4096,256]{2,1,0:T(8,128)(2,1)S(1)}, bf16[2,4096,256]{2,1,0:T(8,128)(2,1)}, u32[]{:S(2)}) copy-start(bf16[2,4096,256]{2,1,0:T(8,128)(2,1)} %up_ref.3) | copy-start | bytes 12582916
  11.6 23.7 %copy-start.1 = (bf16[2,4096,256]{2,1,0:T(8,128)(2,1)S(1)}, bf16[2,4096,256]{2,1,0:T(8,128)(2,1)}, u32[]{:S(2)}) copy-start(bf16[2,4096,256]{2,1,0:T(8,128)(2,1)} %gate_ref.3) | copy-start | bytes 12582916
  13.0 22.2 %copy-start = (bf16[2,256,4096]{2,1,0:T(8,128)(2,1)S(1)}, bf16[2,256,4096]{2,1,0:T(8,128)(2,1)}, u32[]{:S(2)}) copy-start(bf16[2,256,4096]{2,1,0:T(8,128)(2,1)} %down_ref.7) | copy-start | bytes 12582916
  13.0 1.4 %collective-permute-start.3 = (bf16[16,2048]{1,0:T(8,128)(2,1)S(1)}, bf16[16,2048]{1,0:T(8,128)(2,1)S(1)}, u32[]{:S(2)}, u32[]{:S(2)}) collective-permute-start(bf16[16,2048]{1,0:T(8,128)(2,1)S(1)} %get-tuple-element.32), channel_id=1, source_target_pairs={{0,8},{1,9},{2,10},{3,11},{4,12},{5,13},{6,14},{7,15},{8,0},{9,1},... | collective-permute-start | bytes 196616 | tf_op jit(solution)/shard_map/ppermute | solution.py:254
  14.4 4.4 %collective-permute-start.4 = (bf16[16,2048]{1,0:T(8,128)(2,1)S(1)}, bf16[16,2048]{1,0:T(8,128)(2,1)S(1)}, u32[]{:S(2)}, u32[]{:S(2)}) collective-permute-start(bf16[16,2048]{1,0:T(8,128)(2,1)S(1)} %add_convert_fusion.2), channel_id=1, source_target_pairs={{0,16},{1,17},{2,18},{3,19},{4,20},{5,21},{6,22},{7,23},{8,24},{9,... | collective-permute-start | bytes 196616 | tf_op jit(solution)/shard_map/ppermute | solution.py:254
  18.8 6.0 %collective-permute-start.7 = (bf16[16,2176]{1,0:T(8,128)(2,1)S(1)}, bf16[16,2176]{1,0:T(8,128)(2,1)S(1)}, u32[]{:S(2)}, u32[]{:S(2)}) collective-permute-start(bf16[16,2176]{1,0:T(8,128)(2,1)S(1)} %pad_maximum_fusion.2), channel_id=1, source_target_pairs={{0,2},{1,3},{2,0},{3,1},{4,6},{5,7},{6,4},{7,5},{8,10},{9,11},{10,... | collective-permute-start | bytes 208904 | tf_op jit(solution)/shard_map/ppermute | solution.py:254
  20.5 6.8 %collective-permute-start.6 = (bf16[16,2176]{1,0:T(8,128)(2,1)S(1)}, bf16[16,2176]{1,0:T(8,128)(2,1)S(1)}, u32[]{:S(2)}, u32[]{:S(2)}) collective-permute-start(bf16[16,2176]{1,0:T(8,128)(2,1)S(1)} %pad_maximum_fusion.2), channel_id=1, source_target_pairs={{0,4},{1,5},{2,6},{3,7},{4,0},{5,1},{6,2},{7,3},{8,12},{9,13},{10,... | collective-permute-start | bytes 208904 | tf_op jit(solution)/shard_map/ppermute | solution.py:254
  23.1 6.1 %collective-permute-start.5 = (bf16[16,2176]{1,0:T(8,128)(2,1)S(1)}, bf16[16,2176]{1,0:T(8,128)(2,1)S(1)}, u32[]{:S(2)}, u32[]{:S(2)}) collective-permute-start(bf16[16,2176]{1,0:T(8,128)(2,1)S(1)} %pad_maximum_fusion.2), channel_id=1, source_target_pairs={{0,6},{1,7},{2,4},{3,5},{4,2},{5,3},{6,0},{7,1},{8,14},{9,15},{10,... | collective-permute-start | bytes 208904 | tf_op jit(solution)/shard_map/ppermute | solution.py:254
  23.3 7.6 %collective-permute-start.13 = (bf16[16,2176]{1,0:T(8,128)(2,1)S(1)}, bf16[16,2176]{1,0:T(8,128)(2,1)S(1)}, u32[]{:S(2)}, u32[]{:S(2)}) collective-permute-start(bf16[16,2176]{1,0:T(8,128)(2,1)S(1)} %pad_maximum_fusion.2), channel_id=1, source_target_pairs={{0,1},{1,0},{2,3},{3,2},{4,5},{5,4},{6,7},{7,6},{8,9},{9,8},{10,11... | collective-permute-start | bytes 208904 | tf_op jit(solution)/shard_map/ppermute | solution.py:254
  29.2 5.9 %collective-permute-start.14 = (bf16[48,2176]{1,0:T(8,128)(2,1)S(1)}, bf16[48,2176]{1,0:T(8,128)(2,1)S(1)}, u32[]{:S(2)}, u32[]{:S(2)}) collective-permute-start(bf16[48,2176]{1,0:T(8,128)(2,1)S(1)} %pad_maximum_fusion.1), channel_id=1, source_target_pairs={{0,1},{1,0},{2,3},{3,2},{4,5},{5,4},{6,7},{7,6},{8,9},{9,8},{10,11... | collective-permute-start | bytes 626696 | tf_op jit(solution)/shard_map/ppermute | solution.py:254
  30.8 4.4 %collective-permute-start.8 = (bf16[64,2176]{1,0:T(8,128)(2,1)S(1)}, bf16[64,2176]{1,0:T(8,128)(2,1)S(1)}, u32[]{:S(2)}, u32[]{:S(2)}) collective-permute-start(bf16[64,2176]{1,0:T(8,128)(2,1)S(1)} %pad_maximum_fusion.own_ref), channel_id=1, source_target_pairs={{0,8},{1,9},{2,10},{3,11},{4,12},{5,13},{6,14},{7,15},{8,0},{9,1},... | collective-permute-start | bytes 835592 | tf_op jit(solution)/shard_map/ppermute | solution.py:254
  35.1 3.2 %collective-permute-start.15 = (bf16[64,2176]{1,0:T(8,128)(2,1)S(1)}, bf16[64,2176]{1,0:T(8,128)(2,1)S(1)}, u32[]{:S(2)}, u32[]{:S(2)}) collective-permute-start(bf16[64,2176]{1,0:T(8,128)(2,1)S(1)} %constant_dynamic-update-slice_fusion.own_ref), channel_id=1, source_target_pairs={{0,8},{1,9},{2,10},{3,11},{4,12},{5,13},{6,14},{7,15},{8,0},{9,1},... | collective-permute-start | bytes 835592 | tf_op jit(solution)/shard_map/ppermute | solution.py:254
  37.3 3.6 %collective-permute-start.9 = (bf16[64,2048]{1,0:T(8,128)(2,1)S(1)}, bf16[64,2048]{1,0:T(8,128)(2,1)S(1)}, u32[]{:S(2)}, u32[]{:S(2)}) collective-permute-start(bf16[64,2048]{1,0:T(8,128)(2,1)S(1)} %get-tuple-element.34), channel_id=1, source_target_pairs={{0,8},{1,9},{2,10},{3,11},{4,12},{5,13},{6,14},{7,15},{8,0},{9,1},... | collective-permute-start | bytes 786440 | tf_op jit(solution)/shard_map/ppermute | solution.py:254
  40.3 5.1 %collective-permute-start.16 = (bf16[64,2048]{1,0:T(8,128)(2,1)S(1)}, bf16[64,2048]{1,0:T(8,128)(2,1)S(1)}, u32[]{:S(2)}, u32[]{:S(2)}) collective-permute-start(bf16[64,2048]{1,0:T(8,128)(2,1)S(1)} %get-tuple-element.36), channel_id=1, source_target_pairs={{0,8},{1,9},{2,10},{3,11},{4,12},{5,13},{6,14},{7,15},{8,0},{9,1},... | collective-permute-start | bytes 786440 | tf_op jit(solution)/shard_map/ppermute | solution.py:254
  41.0 6.9 %collective-permute-start.10 = (bf16[16,2048]{1,0:T(8,128)(2,1)S(1)}, bf16[16,2048]{1,0:T(8,128)(2,1)S(1)}, u32[]{:S(2)}, u32[]{:S(2)}) collective-permute-start(bf16[16,2048]{1,0:T(8,128)(2,1)S(1)} %get-tuple-element.41), channel_id=1, source_target_pairs={{0,6},{1,7},{2,4},{3,5},{4,2},{5,3},{6,0},{7,1},{8,14},{9,15},{10,... | collective-permute-start | bytes 196616 | tf_op jit(solution)/shard_map/ppermute | solution.py:254
  42.4 7.5 %collective-permute-start.12 = (bf16[16,2048]{1,0:T(8,128)(2,1)S(1)}, bf16[16,2048]{1,0:T(8,128)(2,1)S(1)}, u32[]{:S(2)}, u32[]{:S(2)}) collective-permute-start(bf16[16,2048]{1,0:T(8,128)(2,1)S(1)} %get-tuple-element.42), channel_id=1, source_target_pairs={{0,2},{1,3},{2,0},{3,1},{4,6},{5,7},{6,4},{7,5},{8,10},{9,11},{10,... | collective-permute-start | bytes 196616 | tf_op jit(solution)/shard_map/ppermute | solution.py:254
  42.8 9.7 %collective-permute-start.11 = (bf16[16,2048]{1,0:T(8,128)(2,1)S(1)}, bf16[16,2048]{1,0:T(8,128)(2,1)S(1)}, u32[]{:S(2)}, u32[]{:S(2)}) collective-permute-start(bf16[16,2048]{1,0:T(8,128)(2,1)S(1)} %get-tuple-element.43), channel_id=1, source_target_pairs={{0,4},{1,5},{2,6},{3,7},{4,0},{5,1},{6,2},{7,3},{8,12},{9,13},{10,... | collective-permute-start | bytes 196616 | tf_op jit(solution)/shard_map/ppermute | solution.py:254
  45.5 7.0 %collective-permute-start.17 = (bf16[16,2048]{1,0:T(8,128)(2,1)S(1)}, bf16[16,2048]{1,0:T(8,128)(2,1)S(1)}, u32[]{:S(2)}, u32[]{:S(2)}) collective-permute-start(bf16[16,2048]{1,0:T(8,128)(2,1)S(1)} %get-tuple-element.44), channel_id=1, source_target_pairs={{0,1},{1,0},{2,3},{3,2},{4,5},{5,4},{6,7},{7,6},{8,9},{9,8},{10,11... | collective-permute-start | bytes 196616 | tf_op jit(solution)/shard_map/ppermute | solution.py:254
  47.1 5.8 %collective-permute-start.20 = (bf16[16,2048]{1,0:T(8,128)(2,1)S(1)}, bf16[16,2048]{1,0:T(8,128)(2,1)S(1)}, u32[]{:S(2)}, u32[]{:S(2)}) collective-permute-start(bf16[16,2048]{1,0:T(8,128)(2,1)S(1)} %get-tuple-element.45), channel_id=1, source_target_pairs={{0,3},{1,2},{2,1},{3,0},{4,7},{5,6},{6,5},{7,4},{8,11},{9,10},{10,... | collective-permute-start | bytes 196616 | tf_op jit(solution)/shard_map/ppermute | solution.py:254
  47.9 7.8 %collective-permute-start.19 = (bf16[16,2048]{1,0:T(8,128)(2,1)S(1)}, bf16[16,2048]{1,0:T(8,128)(2,1)S(1)}, u32[]{:S(2)}, u32[]{:S(2)}) collective-permute-start(bf16[16,2048]{1,0:T(8,128)(2,1)S(1)} %get-tuple-element.46), channel_id=1, source_target_pairs={{0,5},{1,4},{2,7},{3,6},{4,1},{5,0},{6,3},{7,2},{8,13},{9,12},{10,... | collective-permute-start | bytes 196616 | tf_op jit(solution)/shard_map/ppermute | solution.py:254
  49.9 7.1 %collective-permute-start.18 = (bf16[16,2048]{1,0:T(8,128)(2,1)S(1)}, bf16[16,2048]{1,0:T(8,128)(2,1)S(1)}, u32[]{:S(2)}, u32[]{:S(2)}) collective-permute-start(bf16[16,2048]{1,0:T(8,128)(2,1)S(1)} %get-tuple-element.47), channel_id=1, source_target_pairs={{0,7},{1,6},{2,5},{3,4},{4,3},{5,2},{6,1},{7,0},{8,15},{9,14},{10,... | collective-permute-start | bytes 196616 | tf_op jit(solution)/shard_map/ppermute | solution.py:254
  57.0 4.3 %collective-permute-start.21 = (bf16[16,2048]{1,0:T(8,128)(2,1)S(1)}, bf16[16,2048]{1,0:T(8,128)(2,1)S(1)}, u32[]{:S(2)}, u32[]{:S(2)}) collective-permute-start(bf16[16,2048]{1,0:T(8,128)(2,1)S(1)} %get-tuple-element.37), channel_id=1, source_target_pairs={{0,16},{1,17},{2,18},{3,19},{4,20},{5,21},{6,22},{7,23},{8,24},{9,... | collective-permute-start | bytes 196616 | tf_op jit(solution)/shard_map/ppermute | solution.py:254
  61.4 1.3 %collective-permute-start.22 = (bf16[16,2048]{1,0:T(8,128)(2,1)S(1)}, bf16[16,2048]{1,0:T(8,128)(2,1)S(1)}, u32[]{:S(2)}, u32[]{:S(2)}) collective-permute-start(bf16[16,2048]{1,0:T(8,128)(2,1)S(1)} %add_convert_fusion.1.mine_ref), channel_id=1, source_target_pairs={{0,8},{1,9},{2,10},{3,11},{4,12},{5,13},{6,14},{7,15},{8,0},{9,1},... | collective-permute-start | bytes 196616 | tf_op jit(solution)/shard_map/ppermute | solution.py:254
where the time goes:
time: 63.5 us; the launch traced here: 63.4 us
  starting transfers between devices  25.9 us (41%)
  waiting for transfers between devices  20.8 us (33%)
  Pallas kernels  15.9 us (25%)
    ppermute x23, starting transfers between devices, swap(): return lax.ppermute(value, ('pool', 'expert'), pairs)  25.9 us
    ppermute x23, waiting for transfers between devices, swap(): return lax.ppermute(value, ('pool', 'expert'), pairs)  20.8 us
    pallas_call x1, Pallas kernels, per_device(): call(functools.partial(cache_kernel, scale), (stat, stat, stat, q_shape,...  7.21 us
    pallas_call x2, Pallas kernels, per_device(): call(expert_kernel, (jax.ShapeDtypeStruct((here, units), bfloat16), jax.S...  4.05 us
    pallas_call x1, Pallas kernels, per_device(): call(functools.partial(page_kernel, heads, rows, scale), (jax.ShapeDtypeS...  1.41 us
  transfers between devices with their start and end apart: 23, of which 11 were waited for; matrix products, arithmetic and copies ran while one was open for 1% of the time, Pallas kernels for 20%

commit v1 on v0

--- a/solution.py
+++ b/solution.py
@@ -49,7 +49,7 @@
 
 def cache_kernel(
     scale, len_hbm, row_hbm, size_hbm, q_hbm, own_ref, kv_hbm, weight_hbm, residual_hbm,
-    acc_ref, top_ref, total_ref, q_ref, owner_ref, send_ref, keep_ref, residual_ref,
+    acc_ref, top_ref, total_ref, q_ref, owner_ref, weight_ref, residual_ref,
     kv_ref, raw_ref, score_ref, low_ref, len_ref, row_ref, size_ref, small_sem, kv_sem, weight_sem,
 ):
     rows, length, kv_heads = kv_hbm.shape[:3]
@@ -67,21 +67,15 @@
     for copy in small:
         copy.start()
     copies = [pltpu.make_async_copy(kv_hbm.at[r, :, head], kv_ref.at[r], kv_sem.at[r]) for r in range(rows)]
-    for copy in copies:
-        copy.start()
-    chunks = weight_sem.shape[1]
-    deep = weight_hbm.shape[0] // chunks
-    half = send_ref.shape[1]
+    half = residual_ref.shape[1]
     mine = pl.ds(pl.multiple_of(core * half, half), half)
-    theirs = pl.ds(pl.multiple_of((1 - core) * half, half), half)
+    chunks = weight_sem.shape[0]
+    part = weight_hbm.shape[0] // chunks
     weights_in = [pltpu.make_async_copy(residual_hbm.at[:, :, mine], raw_ref, small_sem.at[4])]
-    for side, (columns, target) in enumerate(((theirs, send_ref), (mine, keep_ref))):
-        for n in range(chunks):
-            part = pl.ds(n * deep, deep)
-            weights_in.append(
-                pltpu.make_async_copy(weight_hbm.at[part, columns], target.at[part], weight_sem.at[side, n])
-            )
-    for copy in weights_in:
+    for n in range(chunks):
+        rows_of = pl.ds(n * part, part)
+        weights_in.append(pltpu.make_async_copy(weight_hbm.at[rows_of], weight_ref.at[rows_of], weight_sem.at[n]))
+    for copy in weights_in + copies:
         copy.start()
     for copy in small:
         copy.wait()
@@ -162,11 +156,17 @@
         [flat_ref[1, pl.ds(h, tokens, stride=heads), :].astype(bfloat16) for h in range(heads)], axis=1
     )
     low_ref[...] = low
-    send_ref[...] = dot(low, weight_ref[...]).astype(bfloat16)
+    half = send_ref.shape[1]
+    core = lax.axis_index("pool") % cores
+    theirs = pl.ds(pl.multiple_of((1 - core) * half, half), half)
+    send_ref[...] = dot(low, weight_ref[:, theirs]).astype(bfloat16)
 
 
 def project_kernel(low_ref, weight_ref, residual_ref, keep_ref):
-    keep_ref[...] = dot(low_ref[...], weight_ref[...]) + residual_ref[...]
+    half = keep_ref.shape[1]
+    core = lax.axis_index("pool") % cores
+    mine = pl.ds(pl.multiple_of(core * half, half), half)
+    keep_ref[...] = dot(low_ref[...], weight_ref[:, mine]) + residual_ref[...]
 
 
 def expert_kernel(own_ref, other_ref, gate_ref, up_ref, down_ref, act_ref, send_ref):
@@ -281,14 +281,14 @@
     group = steps * heads
     everything = rows * group
     stat = jax.ShapeDtypeStruct((everything, head_dim), float32)
-    weight_half = jax.ShapeDtypeStruct((out_weight.shape[0], half), bfloat16)
     q_shape = jax.ShapeDtypeStruct((everything, head_dim), bfloat16)
     other_lanes = (pool_size - 1) * page_rows
     lanes = 2 * length + page_rows
-    acc, top, total, q, owner, weight_send, weight_keep, own_residual = call(
+    acc, top, total, q, owner, weight, own_residual = call(
         functools.partial(cache_kernel, scale),
         (
-            stat, stat, stat, q_shape, jax.ShapeDtypeStruct((8, other_lanes), jnp.int32), weight_half, weight_half,
+            stat, stat, stat, q_shape, jax.ShapeDtypeStruct((8, other_lanes), jnp.int32),
+            jax.ShapeDtypeStruct(out_weight.shape, bfloat16),
             jax.ShapeDtypeStruct((tokens, half), float32),
         ),
         [HBM] * 4 + [VMEM] + [HBM] * 3,
@@ -302,7 +302,7 @@
             pltpu.SMEM(page_len[:, 0].shape, jnp.int32),
             pltpu.SemaphoreType.DMA((5,)),
             pltpu.SemaphoreType.DMA((rows,)),
-            pltpu.SemaphoreType.DMA((2, 4)),
+            pltpu.SemaphoreType.DMA((8,)),
         ],
         vmem=24,
         flops=4 * everything * lanes * head_dim,
@@ -325,12 +325,12 @@
             pltpu.VMEM((2, everything, head_dim), float32),
         ],
         flops=2 * tokens * heads * head_dim * half,
-    )(q, acc, top, total, owner, *sets[1:], weight_send)
+    )(q, acc, top, total, owner, *sets[1:], weight)
     arrived = swap(send, 1)
     keep = call(
         project_kernel, jax.ShapeDtypeStruct((tokens, half), float32), [VMEM] * 3,
         flops=2 * tokens * heads * head_dim * half,
-    )(low, weight_keep, own_residual)
+    )(low, weight, own_residual)
 
     experts = gate_weight.shape[0] * expert_size
     wide = -(-2 * experts // LANES) * LANES

time: 63.5 us -> 63 us (level)
  no operation moved by 1% of the time
where the time goes in v1:
time: 63 us; the launch traced here: 62.9 us
  starting transfers between devices  25.8 us (41%)
  waiting for transfers between devices  20.9 us (33%)
  Pallas kernels  15.4 us (24%)
    ppermute x23, starting transfers between devices, swap(): return lax.ppermute(value, ('pool', 'expert'), pairs)  25.8 us
    ppermute x23, waiting for transfers between devices, swap(): return lax.ppermute(value, ('pool', 'expert'), pairs)  20.9 us
    pallas_call x1, Pallas kernels, per_device(): call(functools.partial(cache_kernel, scale), (stat, stat, stat, q_shape,...  6.68 us
    pallas_call x2, Pallas kernels, per_device(): call(expert_kernel, (jax.ShapeDtypeStruct((here, units), bfloat16), jax.S...  4.05 us
    pallas_call x1, Pallas kernels, per_device(): call(functools.partial(page_kernel, heads, rows, scale), (jax.ShapeDtypeS...  1.42 us
  transfers between devices with their start and end apart: 23, of which 11 were waited for; matrix products, arithmetic and copies ran while one was open for 1% of the time, Pallas kernels for 20%

profile of v1, /device:TPU:0, one launch (start us, length us, event | category | flops | bytes accessed | tf_op | source)
XLA Modules:
  0.0 62.9 jit_solution(15677779343427539673)
XLA Ops:
  0.0 1.0 %shard_map.127 = (bf16[4,64,2,128]{3,2,1,0:T(2,128)(2,1)S(1)}, bf16[4,64,2,128]{3,2,1,0:T(2,128)(2,1)S(1)}) custom-call(bf16[4,1,64,2,2,128]{5,4,3,2,1,0:T(2,128)(2,1)} %pages_hbm.1), custom_call_target="tpu_custom_call" | custom-call | bytes 262144 | tf_op jit(solution)/shard_map/pallas_call | solution.py:266
  1.0 2.5 %collective-permute-start.2 = (bf16[512,128]{1,0:T(8,128)(2,1)S(1)}, bf16[512,128]{1,0:T(8,128)(2,1)S(1)}, u32[]{:S(2)}, u32[]{:S(2)}) collective-permute-start(bf16[512,128]{1,0:T(8,128)(2,1)S(1)} %bitcast.9), channel_id=1, source_target_pairs={{0,24},{1,25},{2,26},{3,27},{4,28},{5,29},{6,30},{7,31},{8,16},{9,... | collective-permute-start | bytes 393224 | tf_op jit(solution)/shard_map/ppermute | solution.py:254
  3.5 0.6 %collective-permute-start = (bf16[512,128]{1,0:T(8,128)(2,1)S(1)}, bf16[512,128]{1,0:T(8,128)(2,1)S(1)}, u32[]{:S(2)}, u32[]{:S(2)}) collective-permute-start(bf16[512,128]{1,0:T(8,128)(2,1)S(1)} %bitcast.10), channel_id=1, source_target_pairs={{0,16},{1,17},{2,18},{3,19},{4,20},{5,21},{6,22},{7,23},{8,24},{9,... | collective-permute-start | bytes 393224 | tf_op jit(solution)/shard_map/ppermute | solution.py:254
  4.1 0.0 collective-permute-start.1
  4.2 6.7 %shard_map.128 = (f32[128,128]{1,0:T(8,128)S(1)}, f32[128,128]{1,0:T(8,128)S(1)}, f32[128,128]{1,0:T(8,128)S(1)}, bf16[128,128]{1,0:T(8,128)(2,1)S(1)}, s32[8,15...) custom-call(s32[8]{0:T(128)} %len_hbm.1, s32[16]{0:T(128)} %bitcast.14, s32[16]{0:T(128)} %bitcast.15, ...), custom_call_target="tpu_custom_call" | custom-call | flops 100663296 | bytes 10485760 | tf_op jit(solution)/shard_map/pallas_call | solution.py:287
  10.9 0.0 copy-done.3
  10.9 0.0 copy-done.4
  10.9 0.1 select_reduce_fusion
  11.0 0.0 collective-permute-done.2.rest_2_
  11.0 0.0 collective-permute-done.rest_0_
  11.0 0.0 collective-permute-done.1.rest_1_
  11.0 0.0 copy-start.2
  11.0 1.4 %shard_map.129 = (bf16[16,1024]{1,0:T(8,128)(2,1)S(1)}, bf16[16,2048]{1,0:T(8,128)(2,1)S(1)}) custom-call(bf16[128,128]{1,0:T(8,128)(2,1)S(1)} %get-tuple-element.21.q_ref, f32[128,128]{1,0:T(8,128)S(1)} %get-tuple-element.22.acc_in, f32[128,128]{1,0:T(8,128)S(1)} %get-tuple-element.23.top_in, f32[128,128]{1,0:T(8,128)S(1)} %get-tuple-element.24.total_in, ...), custom_call_target="tpu_custom_call" | custom-call | flops 67108864 | tf_op jit(solution)/shard_map/pallas_call | solution.py:315
  12.5 0.5 collective-permute-start.3
  13.0 0.7 %shard_map.130 = f32[16,2048]{1,0:T(8,128)S(1)} custom-call(bf16[16,1024]{1,0:T(8,128)(2,1)S(1)} %get-tuple-element.28.low_ref, bf16[1024,4096]{1,0:T(8,128)(2,1)S(1)} %get-tuple-element.27.rest_3_.weight_ref, f32[16,2048]{1,0:T(8,128)S(1)} %get-tuple-element.29.residual_ref), custom_call_target="tpu_custom_call" | custom-call | flops 67108864 | tf_op jit(solution)/shard_map/pallas_call | solution.py:330
  13.6 0.2 collective-permute-done.3
  13.9 1.7 %collective-permute-start.4 = (bf16[16,2048]{1,0:T(8,128)(2,1)S(1)}, bf16[16,2048]{1,0:T(8,128)(2,1)S(1)}, u32[]{:S(2)}, u32[]{:S(2)}) collective-permute-start(bf16[16,2048]{1,0:T(8,128)(2,1)S(1)} %add_convert_fusion.2), channel_id=1, source_target_pairs={{0,16},{1,17},{2,18},{3,19},{4,20},{5,21},{6,22},{7,23},{8,24},{9,... | collective-permute-start | bytes 196616 | tf_op jit(solution)/shard_map/ppermute | solution.py:254
  15.6 2.7 %collective-permute-done.4 = bf16[16,2048]{1,0:T(8,128)(2,1)S(1)} collective-permute-done((bf16[16,2048]{1,0:T(8,128)(2,1)S(1)}, bf16[16,2048]{1,0:T(8,128)(2,1)S(1)}, u32[]{:S(2)}, u32[]{:S(2)}) %collective-permute-start.4) | collective-permute-done | bytes 65568 | tf_op jit(solution)/shard_map/ppermute | solution.py:254
  18.3 1.7 %collective-permute-start.7 = (bf16[16,2176]{1,0:T(8,128)(2,1)S(1)}, bf16[16,2176]{1,0:T(8,128)(2,1)S(1)}, u32[]{:S(2)}, u32[]{:S(2)}) collective-permute-start(bf16[16,2176]{1,0:T(8,128)(2,1)S(1)} %pad_maximum_fusion.2), channel_id=1, source_target_pairs={{0,2},{1,3},{2,0},{3,1},{4,6},{5,7},{6,4},{7,5},{8,10},{9,11},{10,... | collective-permute-start | bytes 208904 | tf_op jit(solution)/shard_map/ppermute | solution.py:254
  20.0 2.6 %collective-permute-start.6 = (bf16[16,2176]{1,0:T(8,128)(2,1)S(1)}, bf16[16,2176]{1,0:T(8,128)(2,1)S(1)}, u32[]{:S(2)}, u32[]{:S(2)}) collective-permute-start(bf16[16,2176]{1,0:T(8,128)(2,1)S(1)} %pad_maximum_fusion.2), channel_id=1, source_target_pairs={{0,4},{1,5},{2,6},{3,7},{4,0},{5,1},{6,2},{7,3},{8,12},{9,13},{10,... | collective-permute-start | bytes 208904 | tf_op jit(solution)/shard_map/ppermute | solution.py:254
  22.6 0.2 collective-permute-start.5
  22.8 1.5 %collective-permute-start.13 = (bf16[16,2176]{1,0:T(8,128)(2,1)S(1)}, bf16[16,2176]{1,0:T(8,128)(2,1)S(1)}, u32[]{:S(2)}, u32[]{:S(2)}) collective-permute-start(bf16[16,2176]{1,0:T(8,128)(2,1)S(1)} %pad_maximum_fusion.2), channel_id=1, source_target_pairs={{0,1},{1,0},{2,3},{3,2},{4,5},{5,4},{6,7},{7,6},{8,9},{9,8},{10,11... | collective-permute-start | bytes 208904 | tf_op jit(solution)/shard_map/ppermute | solution.py:254
  24.3 0.0 collective-permute-done.7
  24.3 2.5 %collective-permute-done.6 = bf16[16,2176]{1,0:T(8,128)(2,1)S(1)} collective-permute-done((bf16[16,2176]{1,0:T(8,128)(2,1)S(1)}, bf16[16,2176]{1,0:T(8,128)(2,1)S(1)}, u32[]{:S(2)}, u32[]{:S(2)}) %collective-permute-start.6) | collective-permute-done | bytes 69664 | tf_op jit(solution)/shard_map/ppermute | solution.py:254
  26.8 1.9 %collective-permute-done.5 = bf16[16,2176]{1,0:T(8,128)(2,1)S(1)} collective-permute-done((bf16[16,2176]{1,0:T(8,128)(2,1)S(1)}, bf16[16,2176]{1,0:T(8,128)(2,1)S(1)}, u32[]{:S(2)}, u32[]{:S(2)}) %collective-permute-start.5) | collective-permute-done | bytes 69664 | tf_op jit(solution)/shard_map/ppermute | solution.py:254
  28.7 1.6 %collective-permute-start.14 = (bf16[48,2176]{1,0:T(8,128)(2,1)S(1)}, bf16[48,2176]{1,0:T(8,128)(2,1)S(1)}, u32[]{:S(2)}, u32[]{:S(2)}) collective-permute-start(bf16[48,2176]{1,0:T(8,128)(2,1)S(1)} %pad_maximum_fusion.1), channel_id=1, source_target_pairs={{0,1},{1,0},{2,3},{3,2},{4,5},{5,4},{6,7},{7,6},{8,9},{9,8},{10,11... | collective-permute-start | bytes 626696 | tf_op jit(solution)/shard_map/ppermute | solution.py:254
  30.3 0.1 collective-permute-start.8
  30.4 0.0 collective-permute-done.13
  30.4 4.2 %collective-permute-done.14 = bf16[48,2176]{1,0:T(8,128)(2,1)S(1)} collective-permute-done((bf16[48,2176]{1,0:T(8,128)(2,1)S(1)}, bf16[48,2176]{1,0:T(8,128)(2,1)S(1)}, u32[]{:S(2)}, u32[]{:S(2)}) %collective-permute-start.14) | collective-permute-done | bytes 208928 | tf_op jit(solution)/shard_map/ppermute | solution.py:254
  34.6 0.1 collective-permute-start.15
  34.7 0.0 collective-permute-done.8.other_ref
  34.7 0.0 copy-done.2
  34.7 0.0 copy-done
  34.7 2.0 %shard_map.131 = (bf16[64,512]{1,0:T(8,128)(2,1)S(1)}, bf16[64,2048]{1,0:T(8,128)(2,1)S(1)}) custom-call(bf16[64,2176]{1,0:T(8,128)(2,1)S(1)} %pad_maximum_fusion.own_ref, bf16[64,2176]{1,0:T(8,128)(2,1)S(1)} %collective-permute-done.8.other_ref, bf16[2,4096,256]{2,1,0:T(8,128)(2,1)S(1)} %copy-done.1, bf16[2,4096,256]{2,1,0:T(8,128)(2,1)S(1)} %copy-done.2, ...), custom_call_target="tpu_custom_call" | custom-call | flops 671088640 | tf_op jit(solution)/shard_map/pallas_call | solution.py:364
  36.7 0.5 collective-permute-start.9
  37.3 0.5 shard_map.132
  37.8 0.0 collective-permute-done.15.other_ref
  37.8 2.0 %shard_map.133 = (bf16[64,512]{1,0:T(8,128)(2,1)S(1)}, bf16[64,2048]{1,0:T(8,128)(2,1)S(1)}) custom-call(bf16[64,2176]{1,0:T(8,128)(2,1)S(1)} %constant_dynamic-update-slice_fusion.own_ref, bf16[64,2176]{1,0:T(8,128)(2,1)S(1)} %collective-permute-done.15.other_ref, bf16[2,4096,256]{2,1,0:T(8,128)(2,1)S(1)} %copy-done.1, bf16[2,4096,256]{2,1,0:T(8,128)(2,1)S(1)} %copy-done.2, ...), custom_call_target="tpu_custom_call" | custom-call | flops 671088640 | tf_op jit(solution)/shard_map/pallas_call | solution.py:364
  39.8 0.1 collective-permute-start.16
  39.9 0.5 shard_map.134
  40.4 0.0 collective-permute-done.9
  40.4 0.1 fusion.11
  40.5 1.4 %collective-permute-start.10 = (bf16[16,2048]{1,0:T(8,128)(2,1)S(1)}, bf16[16,2048]{1,0:T(8,128)(2,1)S(1)}, u32[]{:S(2)}, u32[]{:S(2)}) collective-permute-start(bf16[16,2048]{1,0:T(8,128)(2,1)S(1)} %get-tuple-element.39), channel_id=1, source_target_pairs={{0,6},{1,7},{2,4},{3,5},{4,2},{5,3},{6,0},{7,1},{8,14},{9,15},{10,... | collective-permute-start | bytes 196616 | tf_op jit(solution)/shard_map/ppermute | solution.py:254
  41.9 0.4 collective-permute-start.12
  42.3 2.7 %collective-permute-start.11 = (bf16[16,2048]{1,0:T(8,128)(2,1)S(1)}, bf16[16,2048]{1,0:T(8,128)(2,1)S(1)}, u32[]{:S(2)}, u32[]{:S(2)}) collective-permute-start(bf16[16,2048]{1,0:T(8,128)(2,1)S(1)} %get-tuple-element.41), channel_id=1, source_target_pairs={{0,4},{1,5},{2,6},{3,7},{4,0},{5,1},{6,2},{7,3},{8,12},{9,13},{10,... | collective-permute-start | bytes 196616 | tf_op jit(solution)/shard_map/ppermute | solution.py:254
  44.9 0.0 collective-permute-done.16
  45.0 0.1 add_convert_fusion
  45.0 1.6 %collective-permute-start.17 = (bf16[16,2048]{1,0:T(8,128)(2,1)S(1)}, bf16[16,2048]{1,0:T(8,128)(2,1)S(1)}, u32[]{:S(2)}, u32[]{:S(2)}) collective-permute-start(bf16[16,2048]{1,0:T(8,128)(2,1)S(1)} %get-tuple-element.42), channel_id=1, source_target_pairs={{0,1},{1,0},{2,3},{3,2},{4,5},{5,4},{6,7},{7,6},{8,9},{9,8},{10,11... | collective-permute-start | bytes 196616 | tf_op jit(solution)/shard_map/ppermute | solution.py:254
  46.6 0.0 collective-permute-start.20
  46.6 0.8 %collective-permute-done.10 = bf16[16,2048]{1,0:T(8,128)(2,1)S(1)} collective-permute-done((bf16[16,2048]{1,0:T(8,128)(2,1)S(1)}, bf16[16,2048]{1,0:T(8,128)(2,1)S(1)}, u32[]{:S(2)}, u32[]{:S(2)}) %collective-permute-start.10) | collective-permute-done | bytes 65568 | tf_op jit(solution)/shard_map/ppermute | solution.py:254
  47.4 2.0 %collective-permute-start.19 = (bf16[16,2048]{1,0:T(8,128)(2,1)S(1)}, bf16[16,2048]{1,0:T(8,128)(2,1)S(1)}, u32[]{:S(2)}, u32[]{:S(2)}) collective-permute-start(bf16[16,2048]{1,0:T(8,128)(2,1)S(1)} %get-tuple-element.44), channel_id=1, source_target_pairs={{0,5},{1,4},{2,7},{3,6},{4,1},{5,0},{6,3},{7,2},{8,13},{9,12},{10,... | collective-permute-start | bytes 196616 | tf_op jit(solution)/shard_map/ppermute | solution.py:254
  49.4 0.0 collective-permute-done.12
  49.4 2.6 %collective-permute-start.18 = (bf16[16,2048]{1,0:T(8,128)(2,1)S(1)}, bf16[16,2048]{1,0:T(8,128)(2,1)S(1)}, u32[]{:S(2)}, u32[]{:S(2)}) collective-permute-start(bf16[16,2048]{1,0:T(8,128)(2,1)S(1)} %get-tuple-element.45), channel_id=1, source_target_pairs={{0,7},{1,6},{2,5},{3,4},{4,3},{5,2},{6,1},{7,0},{8,15},{9,14},{10,... | collective-permute-start | bytes 196616 | tf_op jit(solution)/shard_map/ppermute | solution.py:254
  52.0 0.0 collective-permute-done.11
  52.0 0.0 collective-permute-done.17
  52.0 0.4 collective-permute-done.20
  52.4 2.9 %collective-permute-done.19 = bf16[16,2048]{1,0:T(8,128)(2,1)S(1)} collective-permute-done((bf16[16,2048]{1,0:T(8,128)(2,1)S(1)}, bf16[16,2048]{1,0:T(8,128)(2,1)S(1)}, u32[]{:S(2)}, u32[]{:S(2)}) %collective-permute-start.19) | collective-permute-done | bytes 65568 | tf_op jit(solution)/shard_map/ppermute | solution.py:254
  55.2 1.2 %collective-permute-done.18 = bf16[16,2048]{1,0:T(8,128)(2,1)S(1)} collective-permute-done((bf16[16,2048]{1,0:T(8,128)(2,1)S(1)}, bf16[16,2048]{1,0:T(8,128)(2,1)S(1)}, u32[]{:S(2)}, u32[]{:S(2)}) %collective-permute-start.18) | collective-permute-done | bytes 65568 | tf_op jit(solution)/shard_map/ppermute | solution.py:254
  56.5 0.1 fusion.9
  56.5 1.5 %collective-permute-start.21 = (bf16[16,2048]{1,0:T(8,128)(2,1)S(1)}, bf16[16,2048]{1,0:T(8,128)(2,1)S(1)}, u32[]{:S(2)}, u32[]{:S(2)}) collective-permute-start(bf16[16,2048]{1,0:T(8,128)(2,1)S(1)} %get-tuple-element.35), channel_id=1, source_target_pairs={{0,16},{1,17},{2,18},{3,19},{4,20},{5,21},{6,22},{7,23},{8,24},{9,... | collective-permute-start | bytes 196616 | tf_op jit(solution)/shard_map/ppermute | solution.py:254
  58.0 2.8 %collective-permute-done.21 = bf16[16,2048]{1,0:T(8,128)(2,1)S(1)} collective-permute-done((bf16[16,2048]{1,0:T(8,128)(2,1)S(1)}, bf16[16,2048]{1,0:T(8,128)(2,1)S(1)}, u32[]{:S(2)}, u32[]{:S(2)}) %collective-permute-start.21) | collective-permute-done | bytes 65568 | tf_op jit(solution)/shard_map/ppermute | solution.py:254
  60.9 0.1 collective-permute-start.22
  61.0 1.2 %collective-permute-done.22.theirs_ref = bf16[16,2048]{1,0:T(8,128)(2,1)S(1)} collective-permute-done((bf16[16,2048]{1,0:T(8,128)(2,1)S(1)}, bf16[16,2048]{1,0:T(8,128)(2,1)S(1)}, u32[]{:S(2)}, u32[]{:S(2)}) %collective-permute-start.22) | collective-permute-done | bytes 65568 | tf_op jit(solution)/shard_map/ppermute | solution.py:254
  62.2 0.7 %shard_map.135 = bf16[8,2,4096]{2,1,0:T(2,128)(2,1)} custom-call(bf16[16,2048]{1,0:T(8,128)(2,1)S(1)} %add_convert_fusion.1.mine_ref, bf16[16,2048]{1,0:T(8,128)(2,1)S(1)} %collective-permute-done.22.theirs_ref), custom_call_target="tpu_custom_call" | custom-call | bytes 262144 | tf_op jit(solution)/shard_map/pallas_call | solution.py:386
  (18 shorter events, 0.2 us)
Async XLA Ops:
  1.0 10.0 %collective-permute-start.2 = (bf16[512,128]{1,0:T(8,128)(2,1)S(1)}, bf16[512,128]{1,0:T(8,128)(2,1)S(1)}, u32[]{:S(2)}, u32[]{:S(2)}) collective-permute-start(bf16[512,128]{1,0:T(8,128)(2,1)S(1)} %bitcast.9), channel_id=1, source_target_pairs={{0,24},{1,25},{2,26},{3,27},{4,28},{5,29},{6,30},{7,31},{8,16},{9,... | collective-permute-start | bytes 393224 | tf_op jit(solution)/shard_map/ppermute | solution.py:254
  3.5 7.5 %collective-permute-start = (bf16[512,128]{1,0:T(8,128)(2,1)S(1)}, bf16[512,128]{1,0:T(8,128)(2,1)S(1)}, u32[]{:S(2)}, u32[]{:S(2)}) collective-permute-start(bf16[512,128]{1,0:T(8,128)(2,1)S(1)} %bitcast.10), channel_id=1, source_target_pairs={{0,16},{1,17},{2,18},{3,19},{4,20},{5,21},{6,22},{7,23},{8,24},{9,... | collective-permute-start | bytes 393224 | tf_op jit(solution)/shard_map/ppermute | solution.py:254
  4.1 6.9 %collective-permute-start.1 = (bf16[512,128]{1,0:T(8,128)(2,1)S(1)}, bf16[512,128]{1,0:T(8,128)(2,1)S(1)}, u32[]{:S(2)}, u32[]{:S(2)}) collective-permute-start(bf16[512,128]{1,0:T(8,128)(2,1)S(1)} %bitcast.7), channel_id=1, source_target_pairs={{0,8},{1,9},{2,10},{3,11},{4,12},{5,13},{6,14},{7,15},{8,0},{9,1},... | collective-permute-start | bytes 393224 | tf_op jit(solution)/shard_map/ppermute | solution.py:254
  4.2 6.7 %copy-start.3 = (f32[8,2,8]{2,1,0:T(2,128)S(1)}, f32[8,2,8]{2,1,0:T(2,128)}, u32[]{:S(2)}) copy-start(f32[8,2,8]{2,1,0:T(2,128)} %param.21) | copy-start | bytes 1540
  4.2 6.7 %copy-start.4 = (s32[8,2,8]{2,1,0:T(2,128)S(1)}, s32[8,2,8]{2,1,0:T(2,128)}, u32[]{:S(2)}) copy-start(s32[8,2,8]{2,1,0:T(2,128)} %param.20) | copy-start | bytes 1540
  11.0 23.6 %copy-start.2 = (bf16[2,4096,256]{2,1,0:T(8,128)(2,1)S(1)}, bf16[2,4096,256]{2,1,0:T(8,128)(2,1)}, u32[]{:S(2)}) copy-start(bf16[2,4096,256]{2,1,0:T(8,128)(2,1)} %up_ref.3) | copy-start | bytes 12582916
  12.5 1.4 %collective-permute-start.3 = (bf16[16,2048]{1,0:T(8,128)(2,1)S(1)}, bf16[16,2048]{1,0:T(8,128)(2,1)S(1)}, u32[]{:S(2)}, u32[]{:S(2)}) collective-permute-start(bf16[16,2048]{1,0:T(8,128)(2,1)S(1)} %get-tuple-element.30), channel_id=1, source_target_pairs={{0,8},{1,9},{2,10},{3,11},{4,12},{5,13},{6,14},{7,15},{8,0},{9,1},... | collective-permute-start | bytes 196616 | tf_op jit(solution)/shard_map/ppermute | solution.py:254
  12.9 21.7 %copy-start = (bf16[2,256,4096]{2,1,0:T(8,128)(2,1)S(1)}, bf16[2,256,4096]{2,1,0:T(8,128)(2,1)}, u32[]{:S(2)}) copy-start(bf16[2,256,4096]{2,1,0:T(8,128)(2,1)} %down_ref.7) | copy-start | bytes 12582916
  13.0 21.7 %copy-start.1 = (bf16[2,4096,256]{2,1,0:T(8,128)(2,1)S(1)}, bf16[2,4096,256]{2,1,0:T(8,128)(2,1)}, u32[]{:S(2)}) copy-start(bf16[2,4096,256]{2,1,0:T(8,128)(2,1)} %gate_ref.3) | copy-start | bytes 12582916
  13.9 4.4 %collective-permute-start.4 = (bf16[16,2048]{1,0:T(8,128)(2,1)S(1)}, bf16[16,2048]{1,0:T(8,128)(2,1)S(1)}, u32[]{:S(2)}, u32[]{:S(2)}) collective-permute-start(bf16[16,2048]{1,0:T(8,128)(2,1)S(1)} %add_convert_fusion.2), channel_id=1, source_target_pairs={{0,16},{1,17},{2,18},{3,19},{4,20},{5,21},{6,22},{7,23},{8,24},{9,... | collective-permute-start | bytes 196616 | tf_op jit(solution)/shard_map/ppermute | solution.py:254
  18.3 6.0 %collective-permute-start.7 = (bf16[16,2176]{1,0:T(8,128)(2,1)S(1)}, bf16[16,2176]{1,0:T(8,128)(2,1)S(1)}, u32[]{:S(2)}, u32[]{:S(2)}) collective-permute-start(bf16[16,2176]{1,0:T(8,128)(2,1)S(1)} %pad_maximum_fusion.2), channel_id=1, source_target_pairs={{0,2},{1,3},{2,0},{3,1},{4,6},{5,7},{6,4},{7,5},{8,10},{9,11},{10,... | collective-permute-start | bytes 208904 | tf_op jit(solution)/shard_map/ppermute | solution.py:254
  20.0 6.8 %collective-permute-start.6 = (bf16[16,2176]{1,0:T(8,128)(2,1)S(1)}, bf16[16,2176]{1,0:T(8,128)(2,1)S(1)}, u32[]{:S(2)}, u32[]{:S(2)}) collective-permute-start(bf16[16,2176]{1,0:T(8,128)(2,1)S(1)} %pad_maximum_fusion.2), channel_id=1, source_target_pairs={{0,4},{1,5},{2,6},{3,7},{4,0},{5,1},{6,2},{7,3},{8,12},{9,13},{10,... | collective-permute-start | bytes 208904 | tf_op jit(solution)/shard_map/ppermute | solution.py:254
  22.6 6.1 %collective-permute-start.5 = (bf16[16,2176]{1,0:T(8,128)(2,1)S(1)}, bf16[16,2176]{1,0:T(8,128)(2,1)S(1)}, u32[]{:S(2)}, u32[]{:S(2)}) collective-permute-start(bf16[16,2176]{1,0:T(8,128)(2,1)S(1)} %pad_maximum_fusion.2), channel_id=1, source_target_pairs={{0,6},{1,7},{2,4},{3,5},{4,2},{5,3},{6,0},{7,1},{8,14},{9,15},{10,... | collective-permute-start | bytes 208904 | tf_op jit(solution)/shard_map/ppermute | solution.py:254
  22.8 7.6 %collective-permute-start.13 = (bf16[16,2176]{1,0:T(8,128)(2,1)S(1)}, bf16[16,2176]{1,0:T(8,128)(2,1)S(1)}, u32[]{:S(2)}, u32[]{:S(2)}) collective-permute-start(bf16[16,2176]{1,0:T(8,128)(2,1)S(1)} %pad_maximum_fusion.2), channel_id=1, source_target_pairs={{0,1},{1,0},{2,3},{3,2},{4,5},{5,4},{6,7},{7,6},{8,9},{9,8},{10,11... | collective-permute-start | bytes 208904 | tf_op jit(solution)/shard_map/ppermute | solution.py:254
  28.7 5.9 %collective-permute-start.14 = (bf16[48,2176]{1,0:T(8,128)(2,1)S(1)}, bf16[48,2176]{1,0:T(8,128)(2,1)S(1)}, u32[]{:S(2)}, u32[]{:S(2)}) collective-permute-start(bf16[48,2176]{1,0:T(8,128)(2,1)S(1)} %pad_maximum_fusion.1), channel_id=1, source_target_pairs={{0,1},{1,0},{2,3},{3,2},{4,5},{5,4},{6,7},{7,6},{8,9},{9,8},{10,11... | collective-permute-start | bytes 626696 | tf_op jit(solution)/shard_map/ppermute | solution.py:254
  30.3 4.4 %collective-permute-start.8 = (bf16[64,2176]{1,0:T(8,128)(2,1)S(1)}, bf16[64,2176]{1,0:T(8,128)(2,1)S(1)}, u32[]{:S(2)}, u32[]{:S(2)}) collective-permute-start(bf16[64,2176]{1,0:T(8,128)(2,1)S(1)} %pad_maximum_fusion.own_ref), channel_id=1, source_target_pairs={{0,8},{1,9},{2,10},{3,11},{4,12},{5,13},{6,14},{7,15},{8,0},{9,1},... | collective-permute-start | bytes 835592 | tf_op jit(solution)/shard_map/ppermute | solution.py:254
  34.6 3.2 %collective-permute-start.15 = (bf16[64,2176]{1,0:T(8,128)(2,1)S(1)}, bf16[64,2176]{1,0:T(8,128)(2,1)S(1)}, u32[]{:S(2)}, u32[]{:S(2)}) collective-permute-start(bf16[64,2176]{1,0:T(8,128)(2,1)S(1)} %constant_dynamic-update-slice_fusion.own_ref), channel_id=1, source_target_pairs={{0,8},{1,9},{2,10},{3,11},{4,12},{5,13},{6,14},{7,15},{8,0},{9,1},... | collective-permute-start | bytes 835592 | tf_op jit(solution)/shard_map/ppermute | solution.py:254
  36.7 3.6 %collective-permute-start.9 = (bf16[64,2048]{1,0:T(8,128)(2,1)S(1)}, bf16[64,2048]{1,0:T(8,128)(2,1)S(1)}, u32[]{:S(2)}, u32[]{:S(2)}) collective-permute-start(bf16[64,2048]{1,0:T(8,128)(2,1)S(1)} %get-tuple-element.32), channel_id=1, source_target_pairs={{0,8},{1,9},{2,10},{3,11},{4,12},{5,13},{6,14},{7,15},{8,0},{9,1},... | collective-permute-start | bytes 786440 | tf_op jit(solution)/shard_map/ppermute | solution.py:254
  39.8 5.1 %collective-permute-start.16 = (bf16[64,2048]{1,0:T(8,128)(2,1)S(1)}, bf16[64,2048]{1,0:T(8,128)(2,1)S(1)}, u32[]{:S(2)}, u32[]{:S(2)}) collective-permute-start(bf16[64,2048]{1,0:T(8,128)(2,1)S(1)} %get-tuple-element.34), channel_id=1, source_target_pairs={{0,8},{1,9},{2,10},{3,11},{4,12},{5,13},{6,14},{7,15},{8,0},{9,1},... | collective-permute-start | bytes 786440 | tf_op jit(solution)/shard_map/ppermute | solution.py:254
  40.5 6.9 %collective-permute-start.10 = (bf16[16,2048]{1,0:T(8,128)(2,1)S(1)}, bf16[16,2048]{1,0:T(8,128)(2,1)S(1)}, u32[]{:S(2)}, u32[]{:S(2)}) collective-permute-start(bf16[16,2048]{1,0:T(8,128)(2,1)S(1)} %get-tuple-element.39), channel_id=1, source_target_pairs={{0,6},{1,7},{2,4},{3,5},{4,2},{5,3},{6,0},{7,1},{8,14},{9,15},{10,... | collective-permute-start | bytes 196616 | tf_op jit(solution)/shard_map/ppermute | solution.py:254
  41.9 7.5 %collective-permute-start.12 = (bf16[16,2048]{1,0:T(8,128)(2,1)S(1)}, bf16[16,2048]{1,0:T(8,128)(2,1)S(1)}, u32[]{:S(2)}, u32[]{:S(2)}) collective-permute-start(bf16[16,2048]{1,0:T(8,128)(2,1)S(1)} %get-tuple-element.40), channel_id=1, source_target_pairs={{0,2},{1,3},{2,0},{3,1},{4,6},{5,7},{6,4},{7,5},{8,10},{9,11},{10,... | collective-permute-start | bytes 196616 | tf_op jit(solution)/shard_map/ppermute | solution.py:254
  42.3 9.7 %collective-permute-start.11 = (bf16[16,2048]{1,0:T(8,128)(2,1)S(1)}, bf16[16,2048]{1,0:T(8,128)(2,1)S(1)}, u32[]{:S(2)}, u32[]{:S(2)}) collective-permute-start(bf16[16,2048]{1,0:T(8,128)(2,1)S(1)} %get-tuple-element.41), channel_id=1, source_target_pairs={{0,4},{1,5},{2,6},{3,7},{4,0},{5,1},{6,2},{7,3},{8,12},{9,13},{10,... | collective-permute-start | bytes 196616 | tf_op jit(solution)/shard_map/ppermute | solution.py:254
  45.0 6.9 %collective-permute-start.17 = (bf16[16,2048]{1,0:T(8,128)(2,1)S(1)}, bf16[16,2048]{1,0:T(8,128)(2,1)S(1)}, u32[]{:S(2)}, u32[]{:S(2)}) collective-permute-start(bf16[16,2048]{1,0:T(8,128)(2,1)S(1)} %get-tuple-element.42), channel_id=1, source_target_pairs={{0,1},{1,0},{2,3},{3,2},{4,5},{5,4},{6,7},{7,6},{8,9},{9,8},{10,11... | collective-permute-start | bytes 196616 | tf_op jit(solution)/shard_map/ppermute | solution.py:254
  46.6 5.8 %collective-permute-start.20 = (bf16[16,2048]{1,0:T(8,128)(2,1)S(1)}, bf16[16,2048]{1,0:T(8,128)(2,1)S(1)}, u32[]{:S(2)}, u32[]{:S(2)}) collective-permute-start(bf16[16,2048]{1,0:T(8,128)(2,1)S(1)} %get-tuple-element.43), channel_id=1, source_target_pairs={{0,3},{1,2},{2,1},{3,0},{4,7},{5,6},{6,5},{7,4},{8,11},{9,10},{10,... | collective-permute-start | bytes 196616 | tf_op jit(solution)/shard_map/ppermute | solution.py:254
  47.4 7.8 %collective-permute-start.19 = (bf16[16,2048]{1,0:T(8,128)(2,1)S(1)}, bf16[16,2048]{1,0:T(8,128)(2,1)S(1)}, u32[]{:S(2)}, u32[]{:S(2)}) collective-permute-start(bf16[16,2048]{1,0:T(8,128)(2,1)S(1)} %get-tuple-element.44), channel_id=1, source_target_pairs={{0,5},{1,4},{2,7},{3,6},{4,1},{5,0},{6,3},{7,2},{8,13},{9,12},{10,... | collective-permute-start | bytes 196616 | tf_op jit(solution)/shard_map/ppermute | solution.py:254
  49.4 7.1 %collective-permute-start.18 = (bf16[16,2048]{1,0:T(8,128)(2,1)S(1)}, bf16[16,2048]{1,0:T(8,128)(2,1)S(1)}, u32[]{:S(2)}, u32[]{:S(2)}) collective-permute-start(bf16[16,2048]{1,0:T(8,128)(2,1)S(1)} %get-tuple-element.45), channel_id=1, source_target_pairs={{0,7},{1,6},{2,5},{3,4},{4,3},{5,2},{6,1},{7,0},{8,15},{9,14},{10,... | collective-permute-start | bytes 196616 | tf_op jit(solution)/shard_map/ppermute | solution.py:254
  56.5 4.3 %collective-permute-start.21 = (bf16[16,2048]{1,0:T(8,128)(2,1)S(1)}, bf16[16,2048]{1,0:T(8,128)(2,1)S(1)}, u32[]{:S(2)}, u32[]{:S(2)}) collective-permute-start(bf16[16,2048]{1,0:T(8,128)(2,1)S(1)} %get-tuple-element.35), channel_id=1, source_target_pairs={{0,16},{1,17},{2,18},{3,19},{4,20},{5,21},{6,22},{7,23},{8,24},{9,... | collective-permute-start | bytes 196616 | tf_op jit(solution)/shard_map/ppermute | solution.py:254
  60.9 1.3 %collective-permute-start.22 = (bf16[16,2048]{1,0:T(8,128)(2,1)S(1)}, bf16[16,2048]{1,0:T(8,128)(2,1)S(1)}, u32[]{:S(2)}, u32[]{:S(2)}) collective-permute-start(bf16[16,2048]{1,0:T(8,128)(2,1)S(1)} %add_convert_fusion.1.mine_ref), channel_id=1, source_target_pairs={{0,8},{1,9},{2,10},{3,11},{4,12},{5,13},{6,14},{7,15},{8,0},{9,1},... | collective-permute-start | bytes 196616 | tf_op jit(solution)/shard_map/ppermute | solution.py:254

commit v2 on v1

--- a/solution.py
+++ b/solution.py
@@ -348,6 +348,7 @@
     message = jnp.concatenate([hidden, table], axis=1).astype(bfloat16)
     gate_near, up_near, down_near = gate_weight, up_weight, down_weight
     units = gate_weight.shape[0] * gate_weight.shape[2]
+    first = jnp.where(lax.axis_index("pool") // cores == 0, 1.0, 0.0)
     result = 0.0
     flips = list(range(far - 1, 0, -1))
     same = [message]
@@ -378,11 +379,14 @@
                 part = swap(part.astype(bfloat16), 0, k).astype(float32)
             result = result + part
     outcome = result.astype(bfloat16)
-    result = hidden + result
+    shared = (result + hidden * first).astype(bfloat16)
+    mine = result + hidden
     for k in range(1, outer):
-        result = result + swap(outcome, k * cores).astype(float32)
-    mine = result.astype(bfloat16)
-    theirs = swap(mine, 1)
+        mine = mine + swap(outcome, k * cores).astype(float32)
+    theirs = 0.0
+    for k in range(outer - 1, -1, -1):
+        theirs = theirs + swap(shared, k * cores + 1).astype(float32)
+    mine, theirs = mine.astype(bfloat16), theirs.astype(bfloat16)
     return call(
         finish_kernel, jax.ShapeDtypeStruct(residual.shape, bfloat16), [VMEM] * 2, vmem=4, bytes_accessed=4 * residual.size
     )(mine, theirs)

time: 63 us -> 62.6 us (level)
  waiting for transfers between devices: 20.9 us -> 19.7 us
  starting transfers between devices: 25.8 us -> 26.5 us
    ppermute x23 -> x24, waiting for transfers between devices: 20.9 us -> 19.7 us  [swap(): return lax.ppermute(value, ('pool', 'expert'), pairs)]
    ppermute x23 -> x24, starting transfers between devices: 25.8 us -> 26.5 us  [swap(): return lax.ppermute(value, ('pool', 'expert'), pairs)]
  transfers between devices with their start and end apart: 23 -> 24, of which waited for: 11 -> 11; matrix products, arithmetic and copies ran while one was open for 1% -> 1% of each run, Pallas kernels for 20% -> 20%
where the time goes in v2:
time: 62.6 us; the launch traced here: 62.4 us
  starting transfers between devices  26.5 us (42%)
  waiting for transfers between devices  19.7 us (31%)
  Pallas kernels  15.4 us (25%)
    ppermute x24, starting transfers between devices, swap(): return lax.ppermute(value, ('pool', 'expert'), pairs)  26.5 us
    ppermute x24, waiting for transfers between devices, swap(): return lax.ppermute(value, ('pool', 'expert'), pairs)  19.7 us
    pallas_call x1, Pallas kernels, per_device(): call(functools.partial(cache_kernel, scale), (stat, stat, stat, q_shape,...  6.68 us
    pallas_call x2, Pallas kernels, per_device(): call(expert_kernel, (jax.ShapeDtypeStruct((here, units), bfloat16), jax.S...  4.05 us
    pallas_call x1, Pallas kernels, per_device(): call(functools.partial(page_kernel, heads, rows, scale), (jax.ShapeDtypeS...  1.42 us
  transfers between devices with their start and end apart: 24, of which 11 were waited for; matrix products, arithmetic and copies ran while one was open for 1% of the time, Pallas kernels for 20%

profile of v2, /device:TPU:0, one launch (start us, length us, event | category | flops | bytes accessed | tf_op | source)
XLA Modules:
  0.0 62.4 jit_solution(9284450259416546520)
XLA Ops:
  0.0 1.0 %shard_map.127 = (bf16[4,64,2,128]{3,2,1,0:T(2,128)(2,1)S(1)}, bf16[4,64,2,128]{3,2,1,0:T(2,128)(2,1)S(1)}) custom-call(bf16[4,1,64,2,2,128]{5,4,3,2,1,0:T(2,128)(2,1)} %pages_hbm.1), custom_call_target="tpu_custom_call" | custom-call | bytes 262144 | tf_op jit(solution)/shard_map/pallas_call | solution.py:266
  1.0 2.5 %collective-permute-start.2 = (bf16[512,128]{1,0:T(8,128)(2,1)S(1)}, bf16[512,128]{1,0:T(8,128)(2,1)S(1)}, u32[]{:S(2)}, u32[]{:S(2)}) collective-permute-start(bf16[512,128]{1,0:T(8,128)(2,1)S(1)} %bitcast.9), channel_id=1, source_target_pairs={{0,24},{1,25},{2,26},{3,27},{4,28},{5,29},{6,30},{7,31},{8,16},{9,... | collective-permute-start | bytes 393224 | tf_op jit(solution)/shard_map/ppermute | solution.py:254
  3.5 0.6 %collective-permute-start = (bf16[512,128]{1,0:T(8,128)(2,1)S(1)}, bf16[512,128]{1,0:T(8,128)(2,1)S(1)}, u32[]{:S(2)}, u32[]{:S(2)}) collective-permute-start(bf16[512,128]{1,0:T(8,128)(2,1)S(1)} %bitcast.10), channel_id=1, source_target_pairs={{0,16},{1,17},{2,18},{3,19},{4,20},{5,21},{6,22},{7,23},{8,24},{9,... | collective-permute-start | bytes 393224 | tf_op jit(solution)/shard_map/ppermute | solution.py:254
  4.1 0.0 collective-permute-start.1
  4.2 6.7 %shard_map.128 = (f32[128,128]{1,0:T(8,128)S(1)}, f32[128,128]{1,0:T(8,128)S(1)}, f32[128,128]{1,0:T(8,128)S(1)}, bf16[128,128]{1,0:T(8,128)(2,1)S(1)}, s32[8,15...) custom-call(s32[8]{0:T(128)} %len_hbm.1, s32[16]{0:T(128)} %bitcast.14, s32[16]{0:T(128)} %bitcast.15, ...), custom_call_target="tpu_custom_call" | custom-call | flops 100663296 | bytes 10485760 | tf_op jit(solution)/shard_map/pallas_call | solution.py:287
  10.9 0.0 copy-done.3
  10.9 0.0 copy-done.4
  10.9 0.1 select_reduce_fusion
  11.0 0.0 collective-permute-done.2.rest_2_
  11.0 0.0 collective-permute-done.rest_0_
  11.0 0.0 collective-permute-done.1.rest_1_
  11.0 0.0 copy-start.2
  11.0 1.4 %shard_map.129 = (bf16[16,1024]{1,0:T(8,128)(2,1)S(1)}, bf16[16,2048]{1,0:T(8,128)(2,1)S(1)}) custom-call(bf16[128,128]{1,0:T(8,128)(2,1)S(1)} %get-tuple-element.21.q_ref, f32[128,128]{1,0:T(8,128)S(1)} %get-tuple-element.22.acc_in, f32[128,128]{1,0:T(8,128)S(1)} %get-tuple-element.23.top_in, f32[128,128]{1,0:T(8,128)S(1)} %get-tuple-element.24.total_in, ...), custom_call_target="tpu_custom_call" | custom-call | flops 67108864 | tf_op jit(solution)/shard_map/pallas_call | solution.py:315
  12.5 0.5 collective-permute-start.3
  13.0 0.7 %shard_map.130 = f32[16,2048]{1,0:T(8,128)S(1)} custom-call(bf16[16,1024]{1,0:T(8,128)(2,1)S(1)} %get-tuple-element.28.low_ref, bf16[1024,4096]{1,0:T(8,128)(2,1)S(1)} %get-tuple-element.27.rest_3_.weight_ref, f32[16,2048]{1,0:T(8,128)S(1)} %get-tuple-element.29.residual_ref), custom_call_target="tpu_custom_call" | custom-call | flops 67108864 | tf_op jit(solution)/shard_map/pallas_call | solution.py:330
  13.6 0.2 collective-permute-done.3
  13.9 1.7 %collective-permute-start.4 = (bf16[16,2048]{1,0:T(8,128)(2,1)S(1)}, bf16[16,2048]{1,0:T(8,128)(2,1)S(1)}, u32[]{:S(2)}, u32[]{:S(2)}) collective-permute-start(bf16[16,2048]{1,0:T(8,128)(2,1)S(1)} %add_convert_fusion.4), channel_id=1, source_target_pairs={{0,16},{1,17},{2,18},{3,19},{4,20},{5,21},{6,22},{7,23},{8,24},{9,... | collective-permute-start | bytes 196616 | tf_op jit(solution)/shard_map/ppermute | solution.py:254
  15.6 2.7 %collective-permute-done.4 = bf16[16,2048]{1,0:T(8,128)(2,1)S(1)} collective-permute-done((bf16[16,2048]{1,0:T(8,128)(2,1)S(1)}, bf16[16,2048]{1,0:T(8,128)(2,1)S(1)}, u32[]{:S(2)}, u32[]{:S(2)}) %collective-permute-start.4) | collective-permute-done | bytes 65568 | tf_op jit(solution)/shard_map/ppermute | solution.py:254
  18.3 1.7 %collective-permute-start.7 = (bf16[16,2176]{1,0:T(8,128)(2,1)S(1)}, bf16[16,2176]{1,0:T(8,128)(2,1)S(1)}, u32[]{:S(2)}, u32[]{:S(2)}) collective-permute-start(bf16[16,2176]{1,0:T(8,128)(2,1)S(1)} %pad_maximum_fusion.2), channel_id=1, source_target_pairs={{0,2},{1,3},{2,0},{3,1},{4,6},{5,7},{6,4},{7,5},{8,10},{9,11},{10,... | collective-permute-start | bytes 208904 | tf_op jit(solution)/shard_map/ppermute | solution.py:254
  20.0 2.6 %collective-permute-start.6 = (bf16[16,2176]{1,0:T(8,128)(2,1)S(1)}, bf16[16,2176]{1,0:T(8,128)(2,1)S(1)}, u32[]{:S(2)}, u32[]{:S(2)}) collective-permute-start(bf16[16,2176]{1,0:T(8,128)(2,1)S(1)} %pad_maximum_fusion.2), channel_id=1, source_target_pairs={{0,4},{1,5},{2,6},{3,7},{4,0},{5,1},{6,2},{7,3},{8,12},{9,13},{10,... | collective-permute-start | bytes 208904 | tf_op jit(solution)/shard_map/ppermute | solution.py:254
  22.6 0.2 collective-permute-start.5
  22.8 1.5 %collective-permute-start.13 = (bf16[16,2176]{1,0:T(8,128)(2,1)S(1)}, bf16[16,2176]{1,0:T(8,128)(2,1)S(1)}, u32[]{:S(2)}, u32[]{:S(2)}) collective-permute-start(bf16[16,2176]{1,0:T(8,128)(2,1)S(1)} %pad_maximum_fusion.2), channel_id=1, source_target_pairs={{0,1},{1,0},{2,3},{3,2},{4,5},{5,4},{6,7},{7,6},{8,9},{9,8},{10,11... | collective-permute-start | bytes 208904 | tf_op jit(solution)/shard_map/ppermute | solution.py:254
  24.3 0.0 collective-permute-done.7
  24.3 2.5 %collective-permute-done.6 = bf16[16,2176]{1,0:T(8,128)(2,1)S(1)} collective-permute-done((bf16[16,2176]{1,0:T(8,128)(2,1)S(1)}, bf16[16,2176]{1,0:T(8,128)(2,1)S(1)}, u32[]{:S(2)}, u32[]{:S(2)}) %collective-permute-start.6) | collective-permute-done | bytes 69664 | tf_op jit(solution)/shard_map/ppermute | solution.py:254
  26.8 1.9 %collective-permute-done.5 = bf16[16,2176]{1,0:T(8,128)(2,1)S(1)} collective-permute-done((bf16[16,2176]{1,0:T(8,128)(2,1)S(1)}, bf16[16,2176]{1,0:T(8,128)(2,1)S(1)}, u32[]{:S(2)}, u32[]{:S(2)}) %collective-permute-start.5) | collective-permute-done | bytes 69664 | tf_op jit(solution)/shard_map/ppermute | solution.py:254
  28.7 1.6 %collective-permute-start.14 = (bf16[48,2176]{1,0:T(8,128)(2,1)S(1)}, bf16[48,2176]{1,0:T(8,128)(2,1)S(1)}, u32[]{:S(2)}, u32[]{:S(2)}) collective-permute-start(bf16[48,2176]{1,0:T(8,128)(2,1)S(1)} %pad_maximum_fusion.1), channel_id=1, source_target_pairs={{0,1},{1,0},{2,3},{3,2},{4,5},{5,4},{6,7},{7,6},{8,9},{9,8},{10,11... | collective-permute-start | bytes 626696 | tf_op jit(solution)/shard_map/ppermute | solution.py:254
  30.3 0.1 collective-permute-start.8
  30.4 0.0 collective-permute-done.13
  30.4 4.2 %collective-permute-done.14 = bf16[48,2176]{1,0:T(8,128)(2,1)S(1)} collective-permute-done((bf16[48,2176]{1,0:T(8,128)(2,1)S(1)}, bf16[48,2176]{1,0:T(8,128)(2,1)S(1)}, u32[]{:S(2)}, u32[]{:S(2)}) %collective-permute-start.14) | collective-permute-done | bytes 208928 | tf_op jit(solution)/shard_map/ppermute | solution.py:254
  34.6 0.1 collective-permute-start.15
  34.7 0.0 collective-permute-done.8.other_ref
  34.7 0.0 copy-done.2
  34.7 2.0 %shard_map.131 = (bf16[64,512]{1,0:T(8,128)(2,1)S(1)}, bf16[64,2048]{1,0:T(8,128)(2,1)S(1)}) custom-call(bf16[64,2176]{1,0:T(8,128)(2,1)S(1)} %pad_maximum_fusion.own_ref, bf16[64,2176]{1,0:T(8,128)(2,1)S(1)} %collective-permute-done.8.other_ref, bf16[2,4096,256]{2,1,0:T(8,128)(2,1)S(1)} %copy-done.1, bf16[2,4096,256]{2,1,0:T(8,128)(2,1)S(1)} %copy-done.2, ...), custom_call_target="tpu_custom_call" | custom-call | flops 671088640 | tf_op jit(solution)/shard_map/pallas_call | solution.py:365
  36.7 0.5 collective-permute-start.9
  37.3 0.5 shard_map.132
  37.8 0.0 collective-permute-done.15.other_ref
  37.8 2.0 %shard_map.133 = (bf16[64,512]{1,0:T(8,128)(2,1)S(1)}, bf16[64,2048]{1,0:T(8,128)(2,1)S(1)}) custom-call(bf16[64,2176]{1,0:T(8,128)(2,1)S(1)} %constant_dynamic-update-slice_fusion.own_ref, bf16[64,2176]{1,0:T(8,128)(2,1)S(1)} %collective-permute-done.15.other_ref, bf16[2,4096,256]{2,1,0:T(8,128)(2,1)S(1)} %copy-done.1, bf16[2,4096,256]{2,1,0:T(8,128)(2,1)S(1)} %copy-done.2, ...), custom_call_target="tpu_custom_call" | custom-call | flops 671088640 | tf_op jit(solution)/shard_map/pallas_call | solution.py:365
  39.8 0.1 collective-permute-start.16
  39.9 0.5 shard_map.134
  40.4 0.0 collective-permute-done.9
  40.4 0.1 fusion.10
  40.5 1.4 %collective-permute-start.10 = (bf16[16,2048]{1,0:T(8,128)(2,1)S(1)}, bf16[16,2048]{1,0:T(8,128)(2,1)S(1)}, u32[]{:S(2)}, u32[]{:S(2)}) collective-permute-start(bf16[16,2048]{1,0:T(8,128)(2,1)S(1)} %get-tuple-element.39), channel_id=1, source_target_pairs={{0,6},{1,7},{2,4},{3,5},{4,2},{5,3},{6,0},{7,1},{8,14},{9,15},{10,... | collective-permute-start | bytes 196616 | tf_op jit(solution)/shard_map/ppermute | solution.py:254
  41.9 0.4 collective-permute-start.12
  42.3 2.7 %collective-permute-start.11 = (bf16[16,2048]{1,0:T(8,128)(2,1)S(1)}, bf16[16,2048]{1,0:T(8,128)(2,1)S(1)}, u32[]{:S(2)}, u32[]{:S(2)}) collective-permute-start(bf16[16,2048]{1,0:T(8,128)(2,1)S(1)} %get-tuple-element.41), channel_id=1, source_target_pairs={{0,4},{1,5},{2,6},{3,7},{4,0},{5,1},{6,2},{7,3},{8,12},{9,13},{10,... | collective-permute-start | bytes 196616 | tf_op jit(solution)/shard_map/ppermute | solution.py:254
  44.9 0.0 collective-permute-done.16
  45.0 1.6 %collective-permute-start.17 = (bf16[16,2048]{1,0:T(8,128)(2,1)S(1)}, bf16[16,2048]{1,0:T(8,128)(2,1)S(1)}, u32[]{:S(2)}, u32[]{:S(2)}) collective-permute-start(bf16[16,2048]{1,0:T(8,128)(2,1)S(1)} %get-tuple-element.42), channel_id=1, source_target_pairs={{0,1},{1,0},{2,3},{3,2},{4,5},{5,4},{6,7},{7,6},{8,9},{9,8},{10,11... | collective-permute-start | bytes 196616 | tf_op jit(solution)/shard_map/ppermute | solution.py:254
  46.6 0.0 collective-permute-start.20
  46.6 0.8 %collective-permute-done.10 = bf16[16,2048]{1,0:T(8,128)(2,1)S(1)} collective-permute-done((bf16[16,2048]{1,0:T(8,128)(2,1)S(1)}, bf16[16,2048]{1,0:T(8,128)(2,1)S(1)}, u32[]{:S(2)}, u32[]{:S(2)}) %collective-permute-start.10) | collective-permute-done | bytes 65568 | tf_op jit(solution)/shard_map/ppermute | solution.py:254
  47.4 2.0 %collective-permute-start.19 = (bf16[16,2048]{1,0:T(8,128)(2,1)S(1)}, bf16[16,2048]{1,0:T(8,128)(2,1)S(1)}, u32[]{:S(2)}, u32[]{:S(2)}) collective-permute-start(bf16[16,2048]{1,0:T(8,128)(2,1)S(1)} %get-tuple-element.44), channel_id=1, source_target_pairs={{0,5},{1,4},{2,7},{3,6},{4,1},{5,0},{6,3},{7,2},{8,13},{9,12},{10,... | collective-permute-start | bytes 196616 | tf_op jit(solution)/shard_map/ppermute | solution.py:254
  49.4 0.0 collective-permute-done.12
  49.4 2.6 %collective-permute-start.18 = (bf16[16,2048]{1,0:T(8,128)(2,1)S(1)}, bf16[16,2048]{1,0:T(8,128)(2,1)S(1)}, u32[]{:S(2)}, u32[]{:S(2)}) collective-permute-start(bf16[16,2048]{1,0:T(8,128)(2,1)S(1)} %get-tuple-element.45), channel_id=1, source_target_pairs={{0,7},{1,6},{2,5},{3,4},{4,3},{5,2},{6,1},{7,0},{8,15},{9,14},{10,... | collective-permute-start | bytes 196616 | tf_op jit(solution)/shard_map/ppermute | solution.py:254
  52.0 0.0 collective-permute-done.11
  52.0 0.0 collective-permute-done.17
  52.0 0.3 collective-permute-done.20
  52.3 2.9 %collective-permute-done.19 = bf16[16,2048]{1,0:T(8,128)(2,1)S(1)} collective-permute-done((bf16[16,2048]{1,0:T(8,128)(2,1)S(1)}, bf16[16,2048]{1,0:T(8,128)(2,1)S(1)}, u32[]{:S(2)}, u32[]{:S(2)}) %collective-permute-start.19) | collective-permute-done | bytes 65568 | tf_op jit(solution)/shard_map/ppermute | solution.py:254
  55.2 1.2 %collective-permute-done.18 = bf16[16,2048]{1,0:T(8,128)(2,1)S(1)} collective-permute-done((bf16[16,2048]{1,0:T(8,128)(2,1)S(1)}, bf16[16,2048]{1,0:T(8,128)(2,1)S(1)}, u32[]{:S(2)}, u32[]{:S(2)}) %collective-permute-start.18) | collective-permute-done | bytes 65568 | tf_op jit(solution)/shard_map/ppermute | solution.py:254
  56.4 0.1 add_convert_fusion.2
  56.5 1.5 %collective-permute-start.21 = (bf16[16,2048]{1,0:T(8,128)(2,1)S(1)}, bf16[16,2048]{1,0:T(8,128)(2,1)S(1)}, u32[]{:S(2)}, u32[]{:S(2)}) collective-permute-start(bf16[16,2048]{1,0:T(8,128)(2,1)S(1)} %convert_element_type.81), channel_id=1, source_target_pairs={{0,16},{1,17},{2,18},{3,19},{4,20},{5,21},{6,22},{7,23},{8,24},{9,... | collective-permute-start | bytes 196616 | tf_op jit(solution)/shard_map/ppermute | solution.py:254
  58.0 0.0 collective-permute-start.23
  58.0 0.7 %collective-permute-start.22 = (bf16[16,2048]{1,0:T(8,128)(2,1)S(1)}, bf16[16,2048]{1,0:T(8,128)(2,1)S(1)}, u32[]{:S(2)}, u32[]{:S(2)}) collective-permute-start(bf16[16,2048]{1,0:T(8,128)(2,1)S(1)} %get-tuple-element.35), channel_id=1, source_target_pairs={{0,24},{1,25},{2,26},{3,27},{4,28},{5,29},{6,30},{7,31},{8,16},{9,... | collective-permute-start | bytes 196616 | tf_op jit(solution)/shard_map/ppermute | solution.py:254
  58.7 2.1 %collective-permute-done.21 = bf16[16,2048]{1,0:T(8,128)(2,1)S(1)} collective-permute-done((bf16[16,2048]{1,0:T(8,128)(2,1)S(1)}, bf16[16,2048]{1,0:T(8,128)(2,1)S(1)}, u32[]{:S(2)}, u32[]{:S(2)}) %collective-permute-start.21) | collective-permute-done | bytes 65568 | tf_op jit(solution)/shard_map/ppermute | solution.py:254
  60.9 0.0 collective-permute-done.23
  60.9 0.8 %collective-permute-done.22 = bf16[16,2048]{1,0:T(8,128)(2,1)S(1)} collective-permute-done((bf16[16,2048]{1,0:T(8,128)(2,1)S(1)}, bf16[16,2048]{1,0:T(8,128)(2,1)S(1)}, u32[]{:S(2)}, u32[]{:S(2)}) %collective-permute-start.22) | collective-permute-done | bytes 65568 | tf_op jit(solution)/shard_map/ppermute | solution.py:254
  61.8 0.7 %shard_map.135 = bf16[8,2,4096]{2,1,0:T(2,128)(2,1)} custom-call(bf16[16,2048]{1,0:T(8,128)(2,1)S(1)} %add_convert_fusion.3.mine_ref, bf16[16,2048]{1,0:T(8,128)(2,1)S(1)} %add_convert_fusion.1.theirs_ref), custom_call_target="tpu_custom_call" | custom-call | bytes 262144 | tf_op jit(solution)/shard_map/pallas_call | solution.py:390
  (22 shorter events, 0.3 us)
Async XLA Ops:
  1.0 10.0 %collective-permute-start.2 = (bf16[512,128]{1,0:T(8,128)(2,1)S(1)}, bf16[512,128]{1,0:T(8,128)(2,1)S(1)}, u32[]{:S(2)}, u32[]{:S(2)}) collective-permute-start(bf16[512,128]{1,0:T(8,128)(2,1)S(1)} %bitcast.9), channel_id=1, source_target_pairs={{0,24},{1,25},{2,26},{3,27},{4,28},{5,29},{6,30},{7,31},{8,16},{9,... | collective-permute-start | bytes 393224 | tf_op jit(solution)/shard_map/ppermute | solution.py:254
  3.5 7.5 %collective-permute-start = (bf16[512,128]{1,0:T(8,128)(2,1)S(1)}, bf16[512,128]{1,0:T(8,128)(2,1)S(1)}, u32[]{:S(2)}, u32[]{:S(2)}) collective-permute-start(bf16[512,128]{1,0:T(8,128)(2,1)S(1)} %bitcast.10), channel_id=1, source_target_pairs={{0,16},{1,17},{2,18},{3,19},{4,20},{5,21},{6,22},{7,23},{8,24},{9,... | collective-permute-start | bytes 393224 | tf_op jit(solution)/shard_map/ppermute | solution.py:254
  4.1 6.9 %collective-permute-start.1 = (bf16[512,128]{1,0:T(8,128)(2,1)S(1)}, bf16[512,128]{1,0:T(8,128)(2,1)S(1)}, u32[]{:S(2)}, u32[]{:S(2)}) collective-permute-start(bf16[512,128]{1,0:T(8,128)(2,1)S(1)} %bitcast.7), channel_id=1, source_target_pairs={{0,8},{1,9},{2,10},{3,11},{4,12},{5,13},{6,14},{7,15},{8,0},{9,1},... | collective-permute-start | bytes 393224 | tf_op jit(solution)/shard_map/ppermute | solution.py:254
  4.2 6.7 %copy-start.3 = (f32[8,2,8]{2,1,0:T(2,128)S(1)}, f32[8,2,8]{2,1,0:T(2,128)}, u32[]{:S(2)}) copy-start(f32[8,2,8]{2,1,0:T(2,128)} %param.21) | copy-start | bytes 1540
  4.2 6.7 %copy-start.4 = (s32[8,2,8]{2,1,0:T(2,128)S(1)}, s32[8,2,8]{2,1,0:T(2,128)}, u32[]{:S(2)}) copy-start(s32[8,2,8]{2,1,0:T(2,128)} %param.20) | copy-start | bytes 1540
  11.0 23.6 %copy-start.2 = (bf16[2,4096,256]{2,1,0:T(8,128)(2,1)S(1)}, bf16[2,4096,256]{2,1,0:T(8,128)(2,1)}, u32[]{:S(2)}) copy-start(bf16[2,4096,256]{2,1,0:T(8,128)(2,1)} %up_ref.3) | copy-start | bytes 12582916
  12.5 1.4 %collective-permute-start.3 = (bf16[16,2048]{1,0:T(8,128)(2,1)S(1)}, bf16[16,2048]{1,0:T(8,128)(2,1)S(1)}, u32[]{:S(2)}, u32[]{:S(2)}) collective-permute-start(bf16[16,2048]{1,0:T(8,128)(2,1)S(1)} %get-tuple-element.30), channel_id=1, source_target_pairs={{0,8},{1,9},{2,10},{3,11},{4,12},{5,13},{6,14},{7,15},{8,0},{9,1},... | collective-permute-start | bytes 196616 | tf_op jit(solution)/shard_map/ppermute | solution.py:254
  12.9 21.7 %copy-start = (bf16[2,256,4096]{2,1,0:T(8,128)(2,1)S(1)}, bf16[2,256,4096]{2,1,0:T(8,128)(2,1)}, u32[]{:S(2)}) copy-start(bf16[2,256,4096]{2,1,0:T(8,128)(2,1)} %down_ref.7) | copy-start | bytes 12582916
  13.0 21.7 %copy-start.1 = (bf16[2,4096,256]{2,1,0:T(8,128)(2,1)S(1)}, bf16[2,4096,256]{2,1,0:T(8,128)(2,1)}, u32[]{:S(2)}) copy-start(bf16[2,4096,256]{2,1,0:T(8,128)(2,1)} %gate_ref.3) | copy-start | bytes 12582916
  13.9 4.4 %collective-permute-start.4 = (bf16[16,2048]{1,0:T(8,128)(2,1)S(1)}, bf16[16,2048]{1,0:T(8,128)(2,1)S(1)}, u32[]{:S(2)}, u32[]{:S(2)}) collective-permute-start(bf16[16,2048]{1,0:T(8,128)(2,1)S(1)} %add_convert_fusion.4), channel_id=1, source_target_pairs={{0,16},{1,17},{2,18},{3,19},{4,20},{5,21},{6,22},{7,23},{8,24},{9,... | collective-permute-start | bytes 196616 | tf_op jit(solution)/shard_map/ppermute | solution.py:254
  18.3 6.0 %collective-permute-start.7 = (bf16[16,2176]{1,0:T(8,128)(2,1)S(1)}, bf16[16,2176]{1,0:T(8,128)(2,1)S(1)}, u32[]{:S(2)}, u32[]{:S(2)}) collective-permute-start(bf16[16,2176]{1,0:T(8,128)(2,1)S(1)} %pad_maximum_fusion.2), channel_id=1, source_target_pairs={{0,2},{1,3},{2,0},{3,1},{4,6},{5,7},{6,4},{7,5},{8,10},{9,11},{10,... | collective-permute-start | bytes 208904 | tf_op jit(solution)/shard_map/ppermute | solution.py:254
  20.0 6.8 %collective-permute-start.6 = (bf16[16,2176]{1,0:T(8,128)(2,1)S(1)}, bf16[16,2176]{1,0:T(8,128)(2,1)S(1)}, u32[]{:S(2)}, u32[]{:S(2)}) collective-permute-start(bf16[16,2176]{1,0:T(8,128)(2,1)S(1)} %pad_maximum_fusion.2), channel_id=1, source_target_pairs={{0,4},{1,5},{2,6},{3,7},{4,0},{5,1},{6,2},{7,3},{8,12},{9,13},{10,... | collective-permute-start | bytes 208904 | tf_op jit(solution)/shard_map/ppermute | solution.py:254
  22.6 6.1 %collective-permute-start.5 = (bf16[16,2176]{1,0:T(8,128)(2,1)S(1)}, bf16[16,2176]{1,0:T(8,128)(2,1)S(1)}, u32[]{:S(2)}, u32[]{:S(2)}) collective-permute-start(bf16[16,2176]{1,0:T(8,128)(2,1)S(1)} %pad_maximum_fusion.2), channel_id=1, source_target_pairs={{0,6},{1,7},{2,4},{3,5},{4,2},{5,3},{6,0},{7,1},{8,14},{9,15},{10,... | collective-permute-start | bytes 208904 | tf_op jit(solution)/shard_map/ppermute | solution.py:254
  22.8 7.6 %collective-permute-start.13 = (bf16[16,2176]{1,0:T(8,128)(2,1)S(1)}, bf16[16,2176]{1,0:T(8,128)(2,1)S(1)}, u32[]{:S(2)}, u32[]{:S(2)}) collective-permute-start(bf16[16,2176]{1,0:T(8,128)(2,1)S(1)} %pad_maximum_fusion.2), channel_id=1, source_target_pairs={{0,1},{1,0},{2,3},{3,2},{4,5},{5,4},{6,7},{7,6},{8,9},{9,8},{10,11... | collective-permute-start | bytes 208904 | tf_op jit(solution)/shard_map/ppermute | solution.py:254
  28.7 5.9 %collective-permute-start.14 = (bf16[48,2176]{1,0:T(8,128)(2,1)S(1)}, bf16[48,2176]{1,0:T(8,128)(2,1)S(1)}, u32[]{:S(2)}, u32[]{:S(2)}) collective-permute-start(bf16[48,2176]{1,0:T(8,128)(2,1)S(1)} %pad_maximum_fusion.1), channel_id=1, source_target_pairs={{0,1},{1,0},{2,3},{3,2},{4,5},{5,4},{6,7},{7,6},{8,9},{9,8},{10,11... | collective-permute-start | bytes 626696 | tf_op jit(solution)/shard_map/ppermute | solution.py:254
  30.3 4.4 %collective-permute-start.8 = (bf16[64,2176]{1,0:T(8,128)(2,1)S(1)}, bf16[64,2176]{1,0:T(8,128)(2,1)S(1)}, u32[]{:S(2)}, u32[]{:S(2)}) collective-permute-start(bf16[64,2176]{1,0:T(8,128)(2,1)S(1)} %pad_maximum_fusion.own_ref), channel_id=1, source_target_pairs={{0,8},{1,9},{2,10},{3,11},{4,12},{5,13},{6,14},{7,15},{8,0},{9,1},... | collective-permute-start | bytes 835592 | tf_op jit(solution)/shard_map/ppermute | solution.py:254
  34.6 3.2 %collective-permute-start.15 = (bf16[64,2176]{1,0:T(8,128)(2,1)S(1)}, bf16[64,2176]{1,0:T(8,128)(2,1)S(1)}, u32[]{:S(2)}, u32[]{:S(2)}) collective-permute-start(bf16[64,2176]{1,0:T(8,128)(2,1)S(1)} %constant_dynamic-update-slice_fusion.own_ref), channel_id=1, source_target_pairs={{0,8},{1,9},{2,10},{3,11},{4,12},{5,13},{6,14},{7,15},{8,0},{9,1},... | collective-permute-start | bytes 835592 | tf_op jit(solution)/shard_map/ppermute | solution.py:254
  36.7 3.6 %collective-permute-start.9 = (bf16[64,2048]{1,0:T(8,128)(2,1)S(1)}, bf16[64,2048]{1,0:T(8,128)(2,1)S(1)}, u32[]{:S(2)}, u32[]{:S(2)}) collective-permute-start(bf16[64,2048]{1,0:T(8,128)(2,1)S(1)} %get-tuple-element.32), channel_id=1, source_target_pairs={{0,8},{1,9},{2,10},{3,11},{4,12},{5,13},{6,14},{7,15},{8,0},{9,1},... | collective-permute-start | bytes 786440 | tf_op jit(solution)/shard_map/ppermute | solution.py:254
  39.8 5.1 %collective-permute-start.16 = (bf16[64,2048]{1,0:T(8,128)(2,1)S(1)}, bf16[64,2048]{1,0:T(8,128)(2,1)S(1)}, u32[]{:S(2)}, u32[]{:S(2)}) collective-permute-start(bf16[64,2048]{1,0:T(8,128)(2,1)S(1)} %get-tuple-element.34), channel_id=1, source_target_pairs={{0,8},{1,9},{2,10},{3,11},{4,12},{5,13},{6,14},{7,15},{8,0},{9,1},... | collective-permute-start | bytes 786440 | tf_op jit(solution)/shard_map/ppermute | solution.py:254
  40.5 6.9 %collective-permute-start.10 = (bf16[16,2048]{1,0:T(8,128)(2,1)S(1)}, bf16[16,2048]{1,0:T(8,128)(2,1)S(1)}, u32[]{:S(2)}, u32[]{:S(2)}) collective-permute-start(bf16[16,2048]{1,0:T(8,128)(2,1)S(1)} %get-tuple-element.39), channel_id=1, source_target_pairs={{0,6},{1,7},{2,4},{3,5},{4,2},{5,3},{6,0},{7,1},{8,14},{9,15},{10,... | collective-permute-start | bytes 196616 | tf_op jit(solution)/shard_map/ppermute | solution.py:254
  41.9 7.5 %collective-permute-start.12 = (bf16[16,2048]{1,0:T(8,128)(2,1)S(1)}, bf16[16,2048]{1,0:T(8,128)(2,1)S(1)}, u32[]{:S(2)}, u32[]{:S(2)}) collective-permute-start(bf16[16,2048]{1,0:T(8,128)(2,1)S(1)} %get-tuple-element.40), channel_id=1, source_target_pairs={{0,2},{1,3},{2,0},{3,1},{4,6},{5,7},{6,4},{7,5},{8,10},{9,11},{10,... | collective-permute-start | bytes 196616 | tf_op jit(solution)/shard_map/ppermute | solution.py:254
  42.3 9.7 %collective-permute-start.11 = (bf16[16,2048]{1,0:T(8,128)(2,1)S(1)}, bf16[16,2048]{1,0:T(8,128)(2,1)S(1)}, u32[]{:S(2)}, u32[]{:S(2)}) collective-permute-start(bf16[16,2048]{1,0:T(8,128)(2,1)S(1)} %get-tuple-element.41), channel_id=1, source_target_pairs={{0,4},{1,5},{2,6},{3,7},{4,0},{5,1},{6,2},{7,3},{8,12},{9,13},{10,... | collective-permute-start | bytes 196616 | tf_op jit(solution)/shard_map/ppermute | solution.py:254
  45.0 7.0 %collective-permute-start.17 = (bf16[16,2048]{1,0:T(8,128)(2,1)S(1)}, bf16[16,2048]{1,0:T(8,128)(2,1)S(1)}, u32[]{:S(2)}, u32[]{:S(2)}) collective-permute-start(bf16[16,2048]{1,0:T(8,128)(2,1)S(1)} %get-tuple-element.42), channel_id=1, source_target_pairs={{0,1},{1,0},{2,3},{3,2},{4,5},{5,4},{6,7},{7,6},{8,9},{9,8},{10,11... | collective-permute-start | bytes 196616 | tf_op jit(solution)/shard_map/ppermute | solution.py:254
  46.6 5.8 %collective-permute-start.20 = (bf16[16,2048]{1,0:T(8,128)(2,1)S(1)}, bf16[16,2048]{1,0:T(8,128)(2,1)S(1)}, u32[]{:S(2)}, u32[]{:S(2)}) collective-permute-start(bf16[16,2048]{1,0:T(8,128)(2,1)S(1)} %get-tuple-element.43), channel_id=1, source_target_pairs={{0,3},{1,2},{2,1},{3,0},{4,7},{5,6},{6,5},{7,4},{8,11},{9,10},{10,... | collective-permute-start | bytes 196616 | tf_op jit(solution)/shard_map/ppermute | solution.py:254
  47.4 7.8 %collective-permute-start.19 = (bf16[16,2048]{1,0:T(8,128)(2,1)S(1)}, bf16[16,2048]{1,0:T(8,128)(2,1)S(1)}, u32[]{:S(2)}, u32[]{:S(2)}) collective-permute-start(bf16[16,2048]{1,0:T(8,128)(2,1)S(1)} %get-tuple-element.44), channel_id=1, source_target_pairs={{0,5},{1,4},{2,7},{3,6},{4,1},{5,0},{6,3},{7,2},{8,13},{9,12},{10,... | collective-permute-start | bytes 196616 | tf_op jit(solution)/shard_map/ppermute | solution.py:254
  49.4 7.1 %collective-permute-start.18 = (bf16[16,2048]{1,0:T(8,128)(2,1)S(1)}, bf16[16,2048]{1,0:T(8,128)(2,1)S(1)}, u32[]{:S(2)}, u32[]{:S(2)}) collective-permute-start(bf16[16,2048]{1,0:T(8,128)(2,1)S(1)} %get-tuple-element.45), channel_id=1, source_target_pairs={{0,7},{1,6},{2,5},{3,4},{4,3},{5,2},{6,1},{7,0},{8,15},{9,14},{10,... | collective-permute-start | bytes 196616 | tf_op jit(solution)/shard_map/ppermute | solution.py:254
  56.5 4.3 %collective-permute-start.21 = (bf16[16,2048]{1,0:T(8,128)(2,1)S(1)}, bf16[16,2048]{1,0:T(8,128)(2,1)S(1)}, u32[]{:S(2)}, u32[]{:S(2)}) collective-permute-start(bf16[16,2048]{1,0:T(8,128)(2,1)S(1)} %convert_element_type.81), channel_id=1, source_target_pairs={{0,16},{1,17},{2,18},{3,19},{4,20},{5,21},{6,22},{7,23},{8,24},{9,... | collective-permute-start | bytes 196616 | tf_op jit(solution)/shard_map/ppermute | solution.py:254
  58.0 2.9 %collective-permute-start.23 = (bf16[16,2048]{1,0:T(8,128)(2,1)S(1)}, bf16[16,2048]{1,0:T(8,128)(2,1)S(1)}, u32[]{:S(2)}, u32[]{:S(2)}) collective-permute-start(bf16[16,2048]{1,0:T(8,128)(2,1)S(1)} %get-tuple-element.35), channel_id=1, source_target_pairs={{0,8},{1,9},{2,10},{3,11},{4,12},{5,13},{6,14},{7,15},{8,0},{9,1},... | collective-permute-start | bytes 196616 | tf_op jit(solution)/shard_map/ppermute | solution.py:254
  58.0 3.7 %collective-permute-start.22 = (bf16[16,2048]{1,0:T(8,128)(2,1)S(1)}, bf16[16,2048]{1,0:T(8,128)(2,1)S(1)}, u32[]{:S(2)}, u32[]{:S(2)}) collective-permute-start(bf16[16,2048]{1,0:T(8,128)(2,1)S(1)} %get-tuple-element.35), channel_id=1, source_target_pairs={{0,24},{1,25},{2,26},{3,27},{4,28},{5,29},{6,30},{7,31},{8,16},{9,... | collective-permute-start | bytes 196616 | tf_op jit(solution)/shard_map/ppermute | solution.py:254
